TPU v7x, 256 devices: a whole 4x4x8 slice. The times are simulated.
256 devices in a mesh: blk: 16 (over x_lo, y, core), head: 16 (over x_hi, z).
Axes of the slice: x: 4 (x_hi: 2, x_lo: 2; x = x_hi * 2 + x_lo), y: 4, z: 8, core: 2. Of those that a mesh axis runs over, the one named last changes fastest.
Arguments:
- queries: bfloat16 [32768, 2048], P(('blk', 'head')), may hold values from -6 to 6
- key_rows: bfloat16 [32768, 2048], P(('blk', 'head')), may hold values from -6 to 6
- value_rows: bfloat16 [32768, 2048], P(('blk', 'head')), may hold values from -6 to 6
- w_out: bfloat16 [2048, 2048], P('head'), may hold values from -0.125 to 0.125
- first_key: int32 [32768], P('blk'), may hold values from 0 to 32765, as said below
Outputs:
- mixed: bfloat16 [32768, 2048], P(('blk', 'head'))
Inputs may be any that keep to these rules, and one draw needn't show every extreme that they name: first_key[i] <= max(i - 1, 0) and first_key[i] >= i - 2048; the last bin of each aligned block of 2048 bins has first_key exactly i - 2048 where that is not negative; the next-to-last bin of the sequence has first_key exactly 32765.
All inputs are finite; a program needn't handle non-finite values.
Results may differ from a plain program's by a relative error of at most 0.0055.
Values may be sent and summed in bfloat16 or wider, within the bound.
No kernel may reach another device: no remote copies, remote signals or barrier semaphores. Data moves between devices by JAX's collectives and lax.ppermute only.
A program may use at most 64 MiB of HBM per device.

v0:
```python
import math

import jax
import jax.numpy as jnp
from jax import lax
from jax.experimental import pallas as pl
from jax.experimental.pallas import tpu as pltpu
from jax.sharding import PartitionSpec as P


HEAD_DIM = 64
LANES = 128
TILE = 256


def attend_kernel(low_ref, q_ref, own_ref, prev_ref, o_ref, kbuf, vbuf, s_ref, sem):
    t = pl.program_id(0)
    groups = own_ref.shape[0]

    @pl.when(t == 0)
    def _():
        copies = []
        for j, buf in enumerate((kbuf, vbuf)):
            copies.append(
                pltpu.make_async_copy(prev_ref.at[:, j], buf.at[pl.ds(0, groups)], sem.at[2 * j])
            )
            copies.append(
                pltpu.make_async_copy(
                    own_ref.at[:, 1 + j], buf.at[pl.ds(groups, groups)], sem.at[2 * j + 1]
                )
            )
        for copy in copies:
            copy.start()
        for copy in copies:
            copy.wait()

    rows = q_ref.shape[1]
    per_tile = TILE // rows
    blocks = groups // per_tile + 1
    q = q_ref[...].reshape(TILE, LANES)
    lane = lax.broadcasted_iota(jnp.int32, (TILE, LANES), 1)
    key_lane = lax.broadcasted_iota(jnp.int32, (TILE, TILE), 1)
    key_row = lax.broadcasted_iota(jnp.int32, (TILE, TILE), 0)
    low = jnp.concatenate([low_ref[...]] * (TILE // LANES), axis=1)
    zero = jnp.zeros_like(q)
    factor = math.log2(math.e) * HEAD_DIM ** (-0.5)
    outs = []
    for head in range(2):
        mine = (lane < HEAD_DIM) if head == 0 else (lane >= HEAD_DIM)
        q_head = jnp.where(mine, q, zero)
        largest = None
        for kb in range(blocks):
            keys = kbuf[pl.ds(per_tile * (t + kb), per_tile)].reshape(TILE, LANES)
            s = lax.dot_general(
                q_head, keys, (((1,), (1,)), ((), ())), preferred_element_type=jnp.float32
            )
            allowed = (key_lane + kb * TILE) >= low
            if kb == blocks - 1:
                allowed = allowed & (key_lane <= key_row)
            s = jnp.where(allowed, s, -jnp.inf)
            s_ref[head, kb] = s
            top = jnp.maximum(s[:, :LANES], s[:, LANES:])
            largest = top if largest is None else jnp.maximum(largest, top)
        shift = jnp.max(largest, axis=1, keepdims=True) * factor
        total = None
        acc = None
        for kb in range(blocks):
            values = vbuf[pl.ds(per_tile * (t + kb), per_tile)].reshape(TILE, LANES)
            p = jnp.exp2(s_ref[head, kb] * factor - shift)
            part = p[:, :LANES] + p[:, LANES:]
            total = part if total is None else total + part
            term = jnp.dot(p.astype(jnp.bfloat16), values, preferred_element_type=jnp.float32)
            acc = term if acc is None else acc + term
        outs.append(acc / jnp.sum(total, axis=1, keepdims=True))
    out = jnp.where(lane < HEAD_DIM, outs[0], outs[1])
    o_ref[...] = out.astype(jnp.bfloat16).reshape(o_ref.shape)


def attention(low, own, prev):
    groups, _, rows, _ = own.shape
    per_tile = TILE // rows
    tiles = groups // per_tile
    window = groups * rows + TILE
    return pl.pallas_call(
        attend_kernel,
        grid=(tiles,),
        out_shape=jax.ShapeDtypeStruct((groups, rows, LANES), jnp.bfloat16),
        in_specs=[
            pl.BlockSpec((TILE, LANES), lambda t: (t, 0)),
            pl.BlockSpec((per_tile, None, rows, LANES), lambda t: (t, 0, 0, 0)),
            pl.BlockSpec(memory_space=pl.ANY),
            pl.BlockSpec(memory_space=pl.ANY),
        ],
        out_specs=pl.BlockSpec((per_tile, rows, LANES), lambda t: (t, 0, 0)),
        scratch_shapes=[
            pltpu.VMEM((2 * groups, rows, LANES), jnp.bfloat16),
            pltpu.VMEM((2 * groups, rows, LANES), jnp.bfloat16),
            pltpu.VMEM((2, tiles + 1, TILE, TILE), jnp.float32),
            pltpu.SemaphoreType.DMA((4,)),
        ],
        compiler_params=pltpu.CompilerParams(
            dimension_semantics=("arbitrary",), vmem_limit_bytes=32 << 20
        ),
        cost_estimate=pl.CostEstimate(
            flops=8 * groups * rows * window * LANES,
            bytes_accessed=6 * groups * rows * LANES * 2,
            transcendentals=2 * groups * rows * window,
        ),
        name="attend",
    )(low, own, own, prev)


def project_kernel(ctx_ref, mine_ref, other_ref, o_ref, *, core_axis):
    core = lax.rem(lax.axis_index(core_axis), 2)
    ctx = jnp.concatenate([ctx_ref[i] for i in range(ctx_ref.shape[0])], axis=1)
    for ref, place in ((mine_ref, core), (other_ref, 1 - core)):
        out = jnp.dot(ctx, ref[...], preferred_element_type=jnp.float32)
        o_ref[:, pl.ds(pl.multiple_of(place * LANES, LANES), LANES)] = out.astype(jnp.bfloat16)


def project(ctx, mine, other):
    heads, rows, _ = ctx.shape
    pieces, depth, _ = mine.shape
    width = 2 * pieces * LANES
    piece = pl.BlockSpec((None, depth, LANES), lambda g: (g, 0, 0))
    return pl.pallas_call(
        lambda *refs: project_kernel(*refs, core_axis="blk"),
        grid=(pieces,),
        out_shape=jax.ShapeDtypeStruct((rows, width), jnp.bfloat16),
        in_specs=[pl.BlockSpec((heads, rows, LANES), lambda g: (0, 0, 0)), piece, piece],
        out_specs=pl.BlockSpec((rows, 2 * LANES), lambda g: (0, g)),
        compiler_params=pltpu.CompilerParams(dimension_semantics=("arbitrary",)),
        cost_estimate=pl.CostEstimate(
            flops=2 * rows * depth * width, bytes_accessed=2 * depth * width, transcendentals=0
        ),
        name="project",
    )(ctx, mine, other)


def layer(queries, key_rows, value_rows, w_out, first_key):
    place = lax.axis_index("blk")
    blks = lax.axis_size("blk")
    heads = lax.axis_size("head")
    rows = queries.shape[0]
    span = heads * rows

    column = lax.dynamic_slice(w_out, (0, place * LANES), (w_out.shape[0], LANES))
    split = lambda x: x.reshape(rows, heads, LANES).transpose(1, 0, 2)
    parts = [split(x) for x in (queries, key_rows, value_rows)]
    parts.append(jnp.broadcast_to(column[None], (heads,) + column.shape))
    own = lax.all_to_all(jnp.stack(parts, axis=1), "head", 0, 0, tiled=True)
    prev = lax.ppermute(own[:, 1:3], "blk", [(i, i + 1) for i in range(blks - 1)])
    column = own[:, 3].reshape(heads * w_out.shape[0], LANES)
    plane = [list(range(core, blks, 2)) for core in range(2)]
    mine = lax.all_to_all(
        jnp.broadcast_to(column[None], (blks // 2,) + column.shape),
        "blk",
        0,
        0,
        axis_index_groups=plane,
        tiled=True,
    )
    other = lax.ppermute(mine, "blk", [(i, i ^ 1) for i in range(blks)])

    tile_start = (jnp.arange(span, dtype=jnp.int32) // TILE) * TILE
    low = first_key - (place * span - span) - tile_start
    low = jnp.broadcast_to(low[:, None], (span, LANES))
    ctx = attention(low, own, prev)
    ctx = lax.all_to_all(ctx, "head", 0, 0, tiled=True)
    return project(ctx, mine, other)


def solution(mesh):
    placed = (
        P(("blk", "head"), None),
        P(("blk", "head"), None),
        P(("blk", "head"), None),
        P("head", None),
        P("blk"),
    )
    return jax.shard_map(
        layer, mesh=mesh, in_specs=placed, out_specs=P(("blk", "head"), None), check_vma=False
    )
```

profile of v0, /device:TPU:24, one launch (start us, length us, event | category | flops | bytes accessed | tf_op | source)
XLA Modules:
  0.0 184.9 jit_solution(1685912409904918357)
XLA Ops:
  0.0 0.0 copy-start
  0.0 0.0 copy-start.1
  0.0 0.0 copy-start.2
  0.0 1.4 copy.6
  1.4 0.3 copy.7
  1.7 0.0 copy-done.1
  1.7 0.3 copy.8
  2.0 0.3 copy.9
  2.3 0.0 copy-done.2
  2.3 0.3 copy.10
  2.6 0.3 copy.11
  2.9 0.0 copy-done
  2.9 0.1 stack_broadcast_in_dim.2
  3.0 0.3 pad_maximum_fusion
  3.3 61.7 %all_to_all.15.q_ref.own_ref = bf16[16,4,128,128]{3,2,1,0:T(8,128)(2,1)S(1)} all-to-all(bf16[16,4,128,128]{3,2,1,0:T(8,128)(2,1)S(1)} %pad_maximum_fusion), channel_id=1, replica_groups=mesh['blk'=16,'head'=16] {'head'}, dimensions={0} | all-to-all | bytes 4194304 | tf_op jit(solution)/shard_map/all_to_all | solution.py:151
  65.0 0.5 broadcast_in_dim.16
  65.6 49.4 %all_to_all.16.refs_1_ = bf16[8,2048,128]{2,1,0:T(8,128)(2,1)} all-to-all(bf16[8,2048,128]{2,1,0:T(8,128)(2,1)S(1)} %broadcast_in_dim.16), channel_id=1, replica_groups={{0,32,64,96,128,160,192,224},{16,48,80,112,144,176,208,240},{1,33,65,97..., dimensions={0} | all-to-all | bytes 8388608 | tf_op jit(solution)/shard_map/all_to_all | solution.py:155
  115.0 0.0 copy-start.3
  115.0 0.0 collective-permute-start.1
  115.0 1.1 slice.8
  116.1 2.4 %collective-permute-start = (bf16[16,2,128,128]{3,2,1,0:T(8,128)(2,1)}, bf16[16,2,128,128]{3,2,1,0:T(8,128)(2,1)}, u32[]{:S(2)}, u32[]{:S(2)}) collective-permute-start(bf16[16,2,128,128]{3,2,1,0:T(8,128)(2,1)} %slice.8), channel_id=1, source_target_pairs={{0,16},{16,32},{32,48},{48,64},{64,80},{80,96},{96,112},{112,128},... | collective-permute-start | bytes 3145736 | tf_op jit(solution)/shard_map/ppermute | solution.py:152
  118.5 0.0 copy-done.3
  118.5 14.0 %collective-permute-done.prev_ref = bf16[16,2,128,128]{3,2,1,0:T(8,128)(2,1)} collective-permute-done((bf16[16,2,128,128]{3,2,1,0:T(8,128)(2,1)}, bf16[16,2,128,128]{3,2,1,0:T(8,128)(2,1)}, u32[]{:S(2)}, u32[]{:S(2)}) %collective-permute-start) | collective-permute-done | bytes 1048608 | tf_op jit(solution)/shard_map/ppermute | solution.py:152
  132.5 0.3 broadcast_in_dim.6.low_ref
  132.8 19.2 %attend.1 = bf16[16,128,128]{2,1,0:T(8,128)(2,1)S(1)} custom-call(s32[2048,128]{1,0:T(8,128)S(1)} %broadcast_in_dim.6.low_ref, bf16[16,4,128,128]{3,2,1,0:T(8,128)(2,1)S(1)} %all_to_all.15.q_ref.own_ref, bf16[16,4,128,128]{3,2,1,0:T(8,128)(2,1)S(1)} %all_to_all.15.q_ref.own_ref, bf16[16,2,128,128]{3,2,1,0:T(8,128)(2,1)} %collective-permute-done.prev_ref), custom_call_target="tpu_custom_call" | custom-call | flops 4831838208 | bytes 3145728 | tf_op jit(solution)/shard_map/attend/pallas_call | solution.py:84
  152.0 24.6 %all_to_all.17.refs_0_ = bf16[16,128,128]{2,1,0:T(8,128)(2,1)} all-to-all(bf16[16,128,128]{2,1,0:T(8,128)(2,1)S(1)} %attend.1), channel_id=1, replica_groups=mesh['blk'=16,'head'=16] {'head'}, dimensions={0} | all-to-all | bytes 1048576 | tf_op jit(solution)/shard_map/all_to_all | solution.py:169
  176.6 0.0 collective-permute-done.1.refs_2_
  176.6 8.2 %project.1 = bf16[128,2048]{1,0:T(8,128)(2,1)} custom-call(bf16[16,128,128]{2,1,0:T(8,128)(2,1)} %all_to_all.17.refs_0_, bf16[8,2048,128]{2,1,0:T(8,128)(2,1)} %all_to_all.16.refs_1_, bf16[8,2048,128]{2,1,0:T(8,128)(2,1)} %collective-permute-done.1.refs_2_), custom_call_target="tpu_custom_call" | custom-call | flops 1073741824 | bytes 8388608 | tf_op jit(solution)/shard_map/project/pallas_call | solution.py:126
  (3 shorter events, 0.1 us)
Async XLA Ops:
  0.0 2.9 %copy-start = (bf16[128,2048]{1,0:T(8,128)(2,1)S(1)}, bf16[128,2048]{1,0:T(8,128)(2,1)}, u32[]{:S(2)}) copy-start(bf16[128,2048]{1,0:T(8,128)(2,1)} %param.8) | copy-start | bytes 1572868
  0.0 1.7 copy-start.1
  0.0 2.3 %copy-start.2 = (bf16[128,2048]{1,0:T(8,128)(2,1)S(1)}, bf16[128,2048]{1,0:T(8,128)(2,1)}, u32[]{:S(2)}) copy-start(bf16[128,2048]{1,0:T(8,128)(2,1)} %param.7) | copy-start | bytes 1572868
  115.0 3.5 %copy-start.3 = (s32[2048]{0:T(1024)S(1)}, s32[2048]{0:T(1024)}, u32[]{:S(2)}) copy-start(s32[2048]{0:T(1024)} %param.9) | copy-start | bytes 24580
  115.0 61.7 %collective-permute-start.1 = (bf16[8,2048,128]{2,1,0:T(8,128)(2,1)}, bf16[8,2048,128]{2,1,0:T(8,128)(2,1)}, u32[]{:S(2)}, u32[]{:S(2)}) collective-permute-start(bf16[8,2048,128]{2,1,0:T(8,128)(2,1)} %all_to_all.16.refs_1_), channel_id=1, source_target_pairs={{0,16},{16,0},{32,48},{48,32},{64,80},{80,64},{96,112},{112,96},{1... | collective-permute-start | bytes 12582920 | tf_op jit(solution)/shard_map/ppermute | solution.py:163
  116.1 16.4 %collective-permute-start = (bf16[16,2,128,128]{3,2,1,0:T(8,128)(2,1)}, bf16[16,2,128,128]{3,2,1,0:T(8,128)(2,1)}, u32[]{:S(2)}, u32[]{:S(2)}) collective-permute-start(bf16[16,2,128,128]{3,2,1,0:T(8,128)(2,1)} %slice.8), channel_id=1, source_target_pairs={{0,16},{16,32},{32,48},{48,64},{64,80},{80,96},{96,112},{112,128},... | collective-permute-start | bytes 3145736 | tf_op jit(solution)/shard_map/ppermute | solution.py:152
where the time goes:
time: 185 us
  blocking collectives  136 us (74%)
  Pallas kernels  27.4 us (15%)
  waiting for transfers between devices  14 us (8%)
  local copies, waits for them, and re-layouts  4.96 us (3%)
  starting transfers between devices  2.41 us (1%)
    all_to_all x1, blocking collectives, layer(): own = lax.all_to_all(jnp.stack(parts, axis=1), 'head', 0, 0, tiled=True)  61.7 us
    all_to_all x1, blocking collectives, layer(): lax.all_to_all(jnp.broadcast_to(column[None], (blks // 2,) + column.shape...  49.4 us
    all_to_all x1, blocking collectives, layer(): ctx = lax.all_to_all(ctx, 'head', 0, 0, tiled=True)  24.6 us
    pallas_call x1, Pallas kernels, attention(): pl.pallas_call(attend_kernel, grid=(tiles,), out_shape=jax.ShapeDtypeStru...  19.2 us
    ppermute x1, waiting for transfers between devices, layer(): lax.ppermute(own[:, 1:3], 'blk', [(i, i + 1) for i in range(blks - 1)])  14 us
    pallas_call x1, Pallas kernels, project(): pl.pallas_call(lambda *refs: project_kernel(*refs, core_axis='blk'), grid...  8.23 us
  transfers between devices with their start and end apart: 2, of which 1 were waited for; matrix products, arithmetic and copies ran while one was open for 1% of the time, Pallas kernels for 10%

commit v1 on v0

--- a/solution.py
+++ b/solution.py
@@ -1,3 +1,4 @@
+import functools
 import math
 
 import jax
@@ -6,7 +7,6 @@
 from jax.experimental import pallas as pl
 from jax.experimental.pallas import tpu as pltpu
 from jax.sharding import PartitionSpec as P
-
 
 HEAD_DIM = 64
 LANES = 128
@@ -26,7 +26,7 @@
             )
             copies.append(
                 pltpu.make_async_copy(
-                    own_ref.at[:, 1 + j], buf.at[pl.ds(groups, groups)], sem.at[2 * j + 1]
+                    own_ref.at[:, j], buf.at[pl.ds(groups, groups)], sem.at[2 * j + 1]
                 )
             )
         for copy in copies:
@@ -76,8 +76,8 @@
     o_ref[...] = out.astype(jnp.bfloat16).reshape(o_ref.shape)
 
 
-def attention(low, own, prev):
-    groups, _, rows, _ = own.shape
+def attention(low, query, own, prev):
+    groups, rows, _ = query.shape
     per_tile = TILE // rows
     tiles = groups // per_tile
     window = groups * rows + TILE
@@ -87,7 +87,7 @@
         out_shape=jax.ShapeDtypeStruct((groups, rows, LANES), jnp.bfloat16),
         in_specs=[
             pl.BlockSpec((TILE, LANES), lambda t: (t, 0)),
-            pl.BlockSpec((per_tile, None, rows, LANES), lambda t: (t, 0, 0, 0)),
+            pl.BlockSpec((per_tile, rows, LANES), lambda t: (t, 0, 0)),
             pl.BlockSpec(memory_space=pl.ANY),
             pl.BlockSpec(memory_space=pl.ANY),
         ],
@@ -107,34 +107,50 @@
             transcendentals=2 * groups * rows * window,
         ),
         name="attend",
-    )(low, own, own, prev)
-
-
-def project_kernel(ctx_ref, mine_ref, other_ref, o_ref, *, core_axis):
-    core = lax.rem(lax.axis_index(core_axis), 2)
+    )(low, query, own, prev)
+
+
+def project_kernel(ctx_ref, *refs, shifts):
+    count = 2 * len(shifts)
+    pieces, o_ref, held, sem = refs[:count], refs[count], refs[count + 1], refs[count + 2]
+    copies = [pltpu.make_async_copy(pieces[i], held.at[i], sem.at[i]) for i in range(count)]
+    for copy in copies:
+        copy.start()
+    here = lax.axis_index("blk")
+    core = lax.rem(here, 2)
+    x, y = here // 8, lax.rem(here // 2, 4)
     ctx = jnp.concatenate([ctx_ref[i] for i in range(ctx_ref.shape[0])], axis=1)
-    for ref, place in ((mine_ref, core), (other_ref, 1 - core)):
-        out = jnp.dot(ctx, ref[...], preferred_element_type=jnp.float32)
-        o_ref[:, pl.ds(pl.multiple_of(place * LANES, LANES), LANES)] = out.astype(jnp.bfloat16)
-
-
-def project(ctx, mine, other):
-    heads, rows, _ = ctx.shape
-    pieces, depth, _ = mine.shape
-    width = 2 * pieces * LANES
-    piece = pl.BlockSpec((None, depth, LANES), lambda g: (g, 0, 0))
+    for i, (dx, dy) in enumerate(shifts):
+        pair = 4 * lax.rem(x + dx, 2) + lax.rem(y + 4 - dy, 4)
+        copies[2 * i].wait()
+        copies[2 * i + 1].wait()
+        w = jnp.concatenate([held[2 * i], held[2 * i + 1]], axis=1)
+        out = jnp.dot(ctx, w, preferred_element_type=jnp.float32).astype(jnp.bfloat16)
+        for part, where in ((0, core), (1, 1 - core)):
+            at = pl.multiple_of((2 * pair + where) * LANES, LANES)
+            o_ref[:, pl.ds(at, LANES)] = out[:, part * LANES : (part + 1) * LANES]
+
+
+def project(ctx, pieces, shifts):
+    _, rows, _ = ctx.shape
+    depth = pieces[0].shape[0]
+    width = len(pieces) * LANES
     return pl.pallas_call(
-        lambda *refs: project_kernel(*refs, core_axis="blk"),
-        grid=(pieces,),
+        functools.partial(project_kernel, shifts=shifts),
         out_shape=jax.ShapeDtypeStruct((rows, width), jnp.bfloat16),
-        in_specs=[pl.BlockSpec((heads, rows, LANES), lambda g: (0, 0, 0)), piece, piece],
-        out_specs=pl.BlockSpec((rows, 2 * LANES), lambda g: (0, g)),
-        compiler_params=pltpu.CompilerParams(dimension_semantics=("arbitrary",)),
+        in_specs=[pl.BlockSpec(memory_space=pltpu.VMEM)]
+        + [pl.BlockSpec(memory_space=pl.ANY)] * len(pieces),
+        out_specs=pl.BlockSpec(memory_space=pltpu.VMEM),
+        scratch_shapes=[
+            pltpu.VMEM((len(pieces), depth, LANES), jnp.bfloat16),
+            pltpu.SemaphoreType.DMA((len(pieces),)),
+        ],
+        compiler_params=pltpu.CompilerParams(vmem_limit_bytes=60 << 20),
         cost_estimate=pl.CostEstimate(
             flops=2 * rows * depth * width, bytes_accessed=2 * depth * width, transcendentals=0
         ),
         name="project",
-    )(ctx, mine, other)
+    )(ctx, *pieces)
 
 
 def layer(queries, key_rows, value_rows, w_out, first_key):
@@ -143,31 +159,44 @@
     heads = lax.axis_size("head")
     rows = queries.shape[0]
     span = heads * rows
+    split = lambda x: x.reshape(rows, heads, LANES).transpose(1, 0, 2)
 
     column = lax.dynamic_slice(w_out, (0, place * LANES), (w_out.shape[0], LANES))
-    split = lambda x: x.reshape(rows, heads, LANES).transpose(1, 0, 2)
-    parts = [split(x) for x in (queries, key_rows, value_rows)]
-    parts.append(jnp.broadcast_to(column[None], (heads,) + column.shape))
-    own = lax.all_to_all(jnp.stack(parts, axis=1), "head", 0, 0, tiled=True)
-    prev = lax.ppermute(own[:, 1:3], "blk", [(i, i + 1) for i in range(blks - 1)])
-    column = own[:, 3].reshape(heads * w_out.shape[0], LANES)
-    plane = [list(range(core, blks, 2)) for core in range(2)]
-    mine = lax.all_to_all(
-        jnp.broadcast_to(column[None], (blks // 2,) + column.shape),
-        "blk",
+    kvw = lax.all_to_all(
+        jnp.stack(
+            [
+                split(key_rows),
+                split(value_rows),
+                jnp.broadcast_to(column[None], (heads,) + column.shape),
+            ],
+            axis=1,
+        ),
+        "head",
         0,
         0,
-        axis_index_groups=plane,
         tiled=True,
     )
-    other = lax.ppermute(mine, "blk", [(i, i ^ 1) for i in range(blks)])
+    prev = lax.ppermute(kvw[:, :2], "blk", [(i, i + 1) for i in range(blks - 1)])
+    query = lax.all_to_all(split(queries), "head", 0, 0, tiled=True)
+
+    mine = kvw[:, 2].reshape(heads * w_out.shape[0], LANES)
+    shifts = [(dx, dy) for dy in (0, 1, 3, 2) for dx in (0, 1)]
+    pieces = []
+    for dx, dy in shifts:
+        pairs = []
+        for i in range(blks):
+            x, y, core = i // 8, (i // 2) % 4, i % 2
+            pairs.append((i, (x ^ dx) * 8 + ((y + dy) % 4) * 2 + core))
+        piece = mine if dx == dy == 0 else lax.ppermute(mine, "blk", pairs)
+        other = lax.ppermute(piece, "blk", [(i, i ^ 1) for i in range(blks)])
+        pieces += [piece, other]
 
     tile_start = (jnp.arange(span, dtype=jnp.int32) // TILE) * TILE
     low = first_key - (place * span - span) - tile_start
     low = jnp.broadcast_to(low[:, None], (span, LANES))
-    ctx = attention(low, own, prev)
+    ctx = attention(low, query, kvw, prev)
     ctx = lax.all_to_all(ctx, "head", 0, 0, tiled=True)
-    return project(ctx, mine, other)
+    return project(ctx, pieces, shifts)
 
 
 def solution(mesh):

time: 185 us -> 175 us (0.946)
  the two profiles are of different devices: /device:TPU:24 before, /device:TPU:2 now
where the time goes in v1:
time: 175 us; the launch traced here: 174 us
  blocking collectives  49.6 us (28%)
  starting transfers between devices  45.8 us (26%)
  waiting for transfers between devices  45.2 us (26%)
  Pallas kernels  26.4 us (15%)
  local copies, waits for them, and re-layouts  6.88 us (4%)
    all_to_all x1, blocking collectives, layer(): lax.all_to_all(jnp.stack([split(key_rows), split(value_rows), jnp.broadca...  49.6 us
    ppermute x7, waiting for transfers between devices, layer(): piece = mine if dx == dy == 0 else lax.ppermute(mine, 'blk', pairs)  29.5 us
    pallas_call x1, Pallas kernels, attention(): pl.pallas_call(attend_kernel, grid=(tiles,), out_shape=jax.ShapeDtypeStru...  19.8 us
    ppermute x8, starting transfers between devices, layer(): other = lax.ppermute(piece, 'blk', [(i, i ^ 1) for i in range(blks)])  18.9 us
    all_to_all x1, waiting for transfers between devices, layer(): ctx = lax.all_to_all(ctx, 'head', 0, 0, tiled=True)  11.8 us
    all_to_all x1, starting transfers between devices, layer(): ctx = lax.all_to_all(ctx, 'head', 0, 0, tiled=True)  11.7 us
    ppermute x7, starting transfers between devices, layer(): piece = mine if dx == dy == 0 else lax.ppermute(mine, 'blk', pairs)  9.05 us
    pallas_call x1, Pallas kernels, project(): pl.pallas_call(functools.partial(project_kernel, shifts=shifts), out_shap...  6.6 us
  transfers between devices with their start and end apart: 18, of which 8 were waited for; matrix products, arithmetic and copies ran while one was open for 2% of the time, Pallas kernels for 11%

profile of v1, /device:TPU:2, one launch (start us, length us, event | category | flops | bytes accessed | tf_op | source)
XLA Modules:
  0.0 174.5 jit_solution(16347570901628251191)
XLA Ops:
  0.0 1.4 copy.8
  1.4 0.3 copy.9
  1.7 0.3 copy.10
  2.0 0.3 copy.11
  2.6 49.6 %all_to_all.15.own_ref = bf16[16,3,128,128]{3,2,1,0:T(8,128)(2,1)S(1)} all-to-all(bf16[16,3,128,128]{3,2,1,0:T(8,128)(2,1)S(1)} %pad_maximum_fusion), channel_id=1, replica_groups=mesh['blk'=16,'head'=16] {'head'}, dimensions={0} | all-to-all | bytes 3145728 | tf_op jit(solution)/shard_map/all_to_all | solution.py:165
  52.2 4.0 %collective-permute-start.10 = (bf16[2048,128]{1,0:T(8,128)(2,1)S(1)}, bf16[2048,128]{1,0:T(8,128)(2,1)}, u32[]{:S(2)}, u32[]{:S(2)}) collective-permute-start(bf16[2048,128]{1,0:T(8,128)(2,1)S(1)} %bitcast.11), channel_id=1, source_target_pairs={{0,224},{16,240},{32,128},{48,144},{64,160},{80,176},{96,192},{112... | collective-permute-start | bytes 1572872 | tf_op jit(solution)/shard_map/ppermute | solution.py:190
  56.2 1.0 slice.8
  57.2 2.0 %collective-permute-start = (bf16[16,2,128,128]{3,2,1,0:T(8,128)(2,1)}, bf16[16,2,128,128]{3,2,1,0:T(8,128)(2,1)}, u32[]{:S(2)}, u32[]{:S(2)}) collective-permute-start(bf16[16,2,128,128]{3,2,1,0:T(8,128)(2,1)} %slice.8), channel_id=1, source_target_pairs={{0,16},{16,32},{32,48},{48,64},{64,80},{80,96},{96,112},{112,128},... | collective-permute-start | bytes 3145736 | tf_op jit(solution)/shard_map/ppermute | solution.py:179
  59.3 1.3 copy.6
  60.6 1.0 copy.7
  61.6 4.2 %all-to-all-start = ((bf16[16,128,128]{2,1,0:T(8,128)(2,1)}), bf16[16,128,128]{2,1,0:T(8,128)(2,1)S(1)}, u32[]{:S(2)}, u32[]{:S(2)}) async-start(bf16[16,128,128]{2,1,0:T(8,128)(2,1)} %bitcast.20), calls=%async_computation | async-start | bytes 1048576 | tf_op jit(solution)/shard_map/all_to_all | solution.py:180
  65.8 0.7 collective-permute-start.12
  66.5 4.3 %collective-permute-start.14 = (bf16[2048,128]{1,0:T(8,128)(2,1)S(1)}, bf16[2048,128]{1,0:T(8,128)(2,1)}, u32[]{:S(2)}, u32[]{:S(2)}) collective-permute-start(bf16[2048,128]{1,0:T(8,128)(2,1)S(1)} %bitcast.13), channel_id=1, source_target_pairs={{0,192},{16,208},{32,224},{48,240},{64,128},{80,144},{96,160},{112... | collective-permute-start | bytes 1572872 | tf_op jit(solution)/shard_map/ppermute | solution.py:190
  70.9 27.5 %collective-permute-done.12.refs_12_ = bf16[2048,128]{1,0:T(8,128)(2,1)} collective-permute-done((bf16[2048,128]{1,0:T(8,128)(2,1)S(1)}, bf16[2048,128]{1,0:T(8,128)(2,1)}, u32[]{:S(2)}, u32[]{:S(2)}) %collective-permute-start.12) | collective-permute-done | bytes 524320 | tf_op jit(solution)/shard_map/ppermute | solution.py:190
  98.4 17.0 %collective-permute-start.1 = (bf16[2048,128]{1,0:T(8,128)(2,1)S(1)}, bf16[2048,128]{1,0:T(8,128)(2,1)}, u32[]{:S(2)}, u32[]{:S(2)}) collective-permute-start(bf16[2048,128]{1,0:T(8,128)(2,1)S(1)} %bitcast.18), channel_id=1, source_target_pairs={{0,16},{16,0},{32,48},{48,32},{64,80},{80,64},{96,112},{112,96},{1... | collective-permute-start | bytes 1572872 | tf_op jit(solution)/shard_map/ppermute | solution.py:191
  115.4 2.0 %collective-permute-done.4.refs_4_ = bf16[2048,128]{1,0:T(8,128)(2,1)} collective-permute-done((bf16[2048,128]{1,0:T(8,128)(2,1)S(1)}, bf16[2048,128]{1,0:T(8,128)(2,1)}, u32[]{:S(2)}, u32[]{:S(2)}) %collective-permute-start.4) | collective-permute-done | bytes 524320 | tf_op jit(solution)/shard_map/ppermute | solution.py:190
  117.5 0.5 collective-permute-start.13
  118.0 0.3 broadcast_in_dim.2.low_ref
  118.3 19.8 %attend.1 = bf16[16,128,128]{2,1,0:T(8,128)(2,1)} custom-call(s32[2048,128]{1,0:T(8,128)S(1)} %broadcast_in_dim.2.low_ref, bf16[16,128,128]{2,1,0:T(8,128)(2,1)S(1)} %all-to-all-done.q_ref, bf16[16,3,128,128]{3,2,1,0:T(8,128)(2,1)S(1)} %all_to_all.15.own_ref, bf16[16,2,128,128]{3,2,1,0:T(8,128)(2,1)} %collective-permute-done.prev_ref), custom_call_target="tpu_custom_call" | custom-call | flops 4831838208 | bytes 3145728 | tf_op jit(solution)/shard_map/attend/pallas_call | solution.py:84
  138.1 11.7 %all-to-all-start.2 = ((bf16[16,128,128]{2,1,0:T(8,128)(2,1)}), bf16[16,128,128]{2,1,0:T(8,128)(2,1)S(1)}, u32[]{:S(2)}, u32[]{:S(2)}) async-start(bf16[16,128,128]{2,1,0:T(8,128)(2,1)} %attend.1), calls=%async_computation.2 | async-start | bytes 1048576 | tf_op jit(solution)/shard_map/all_to_all | solution.py:198
  149.9 0.5 collective-permute-start.3
  150.4 0.3 collective-permute-start.5
  150.7 0.2 collective-permute-start.7
  150.9 0.3 collective-permute-start.9
  151.2 0.8 collective-permute-done.15.refs_15_
  152.0 0.7 collective-permute-done.3.refs_3_
  152.7 0.7 collective-permute-done.5.refs_5_
  153.5 0.7 collective-permute-done.7.refs_7_
  154.2 0.9 collective-permute-done.9.refs_9_
  155.1 11.8 %all-to-all-done.2.ctx_ref = bf16[16,128,128]{2,1,0:T(8,128)(2,1)S(1)} async-done(((bf16[16,128,128]{2,1,0:T(8,128)(2,1)}), bf16[16,128,128]{2,1,0:T(8,128)(2,1)S(1)}, u32[]{:S(2)}, u32[]{:S(2)}) %all-to-all-start.2) | async-done | bytes 524320 | tf_op jit(solution)/shard_map/all_to_all | solution.py:198
  166.9 0.8 copy-done.2
  167.7 6.6 %project.1 = bf16[128,2048]{1,0:T(8,128)(2,1)} custom-call(bf16[16,128,128]{2,1,0:T(8,128)(2,1)} %copy-done.2, bf16[2048,128]{1,0:T(8,128)(2,1)} %bitcast.19, bf16[2048,128]{1,0:T(8,128)(2,1)} %collective-permute-done.1.refs_1_, bf16[2048,128]{1,0:T(8,128)(2,1)} %collective-permute-done.2.refs_2_, bf16[2048,128]{1,0:T(8,128)(2,1)} %copy-done.4, ...), custom_call_target="tpu_custom_call" | custom-call | flops 1073741824 | bytes 8388608 | tf_op jit(solution)/shard_map/project/pallas_call | solution.py:138
  (38 shorter events, 0.6 us)
Async XLA Ops:
  0.0 2.3 %copy-start = (bf16[128,2048]{1,0:T(8,128)(2,1)S(1)}, bf16[128,2048]{1,0:T(8,128)(2,1)}, u32[]{:S(2)}) copy-start(bf16[128,2048]{1,0:T(8,128)(2,1)} %param.8) | copy-start | bytes 1572868
  0.0 1.7 copy-start.7
  52.2 46.2 %copy-start.1 = (bf16[16,1,128,128]{3,2,1,0:T(8,128)(2,1)}, bf16[16,1,128,128]{3,2,1,0:T(8,128)(2,1)S(1)}, u32[]{:S(2)}) copy-start(bf16[16,1,128,128]{3,2,1,0:T(8,128)(2,1)S(1)} %slice.9) | copy-start | bytes 1572868
  52.2 18.7 %collective-permute-start.10 = (bf16[2048,128]{1,0:T(8,128)(2,1)S(1)}, bf16[2048,128]{1,0:T(8,128)(2,1)}, u32[]{:S(2)}, u32[]{:S(2)}) collective-permute-start(bf16[2048,128]{1,0:T(8,128)(2,1)S(1)} %bitcast.11), channel_id=1, source_target_pairs={{0,224},{16,240},{32,128},{48,144},{64,160},{80,176},{96,192},{112... | collective-permute-start | bytes 1572872 | tf_op jit(solution)/shard_map/ppermute | solution.py:190
  57.2 13.7 %copy-start.8 = (s32[2048]{0:T(1024)S(1)}, s32[2048]{0:T(1024)}, u32[]{:S(2)}) copy-start(s32[2048]{0:T(1024)} %param.9) | copy-start | bytes 24580
  57.2 60.2 %collective-permute-start = (bf16[16,2,128,128]{3,2,1,0:T(8,128)(2,1)}, bf16[16,2,128,128]{3,2,1,0:T(8,128)(2,1)}, u32[]{:S(2)}, u32[]{:S(2)}) collective-permute-start(bf16[16,2,128,128]{3,2,1,0:T(8,128)(2,1)} %slice.8), channel_id=1, source_target_pairs={{0,16},{16,32},{32,48},{48,64},{64,80},{80,96},{96,112},{112,128},... | collective-permute-start | bytes 3145736 | tf_op jit(solution)/shard_map/ppermute | solution.py:179
  61.6 56.4 %all-to-all-start = ((bf16[16,128,128]{2,1,0:T(8,128)(2,1)}), bf16[16,128,128]{2,1,0:T(8,128)(2,1)S(1)}, u32[]{:S(2)}, u32[]{:S(2)}) async-start(bf16[16,128,128]{2,1,0:T(8,128)(2,1)} %bitcast.20), calls=%async_computation | async-start | bytes 1048576 | tf_op jit(solution)/shard_map/all_to_all | solution.py:180
  65.8 32.6 %collective-permute-start.12 = (bf16[2048,128]{1,0:T(8,128)(2,1)S(1)}, bf16[2048,128]{1,0:T(8,128)(2,1)}, u32[]{:S(2)}, u32[]{:S(2)}) collective-permute-start(bf16[2048,128]{1,0:T(8,128)(2,1)S(1)} %bitcast.12), channel_id=1, source_target_pairs={{0,64},{16,80},{32,96},{48,112},{64,0},{80,16},{96,32},{112,48},{1... | collective-permute-start | bytes 1572872 | tf_op jit(solution)/shard_map/ppermute | solution.py:190
  66.5 31.9 %collective-permute-start.14 = (bf16[2048,128]{1,0:T(8,128)(2,1)S(1)}, bf16[2048,128]{1,0:T(8,128)(2,1)}, u32[]{:S(2)}, u32[]{:S(2)}) collective-permute-start(bf16[2048,128]{1,0:T(8,128)(2,1)S(1)} %bitcast.13), channel_id=1, source_target_pairs={{0,192},{16,208},{32,224},{48,240},{64,128},{80,144},{96,160},{112... | collective-permute-start | bytes 1572872 | tf_op jit(solution)/shard_map/ppermute | solution.py:190
  70.8 27.6 %collective-permute-start.2 = (bf16[2048,128]{1,0:T(8,128)(2,1)S(1)}, bf16[2048,128]{1,0:T(8,128)(2,1)}, u32[]{:S(2)}, u32[]{:S(2)}) collective-permute-start(bf16[2048,128]{1,0:T(8,128)(2,1)S(1)} %bitcast.14), channel_id=1, source_target_pairs={{0,128},{16,144},{32,160},{48,176},{64,192},{80,208},{96,224},{112... | collective-permute-start | bytes 1572872 | tf_op jit(solution)/shard_map/ppermute | solution.py:190
  70.9 46.5 %collective-permute-start.4 = (bf16[2048,128]{1,0:T(8,128)(2,1)S(1)}, bf16[2048,128]{1,0:T(8,128)(2,1)}, u32[]{:S(2)}, u32[]{:S(2)}) collective-permute-start(bf16[2048,128]{1,0:T(8,128)(2,1)S(1)} %bitcast.15), channel_id=1, source_target_pairs={{0,32},{16,48},{32,64},{48,80},{64,96},{80,112},{96,0},{112,16},{1... | collective-permute-start | bytes 1572872 | tf_op jit(solution)/shard_map/ppermute | solution.py:190
  98.4 51.4 %collective-permute-start.6 = (bf16[2048,128]{1,0:T(8,128)(2,1)S(1)}, bf16[2048,128]{1,0:T(8,128)(2,1)}, u32[]{:S(2)}, u32[]{:S(2)}) collective-permute-start(bf16[2048,128]{1,0:T(8,128)(2,1)S(1)} %bitcast.16), channel_id=1, source_target_pairs={{0,160},{16,176},{32,192},{48,208},{64,224},{80,240},{96,128},{112... | collective-permute-start | bytes 1572872 | tf_op jit(solution)/shard_map/ppermute | solution.py:190
  98.4 51.5 %collective-permute-start.8 = (bf16[2048,128]{1,0:T(8,128)(2,1)S(1)}, bf16[2048,128]{1,0:T(8,128)(2,1)}, u32[]{:S(2)}, u32[]{:S(2)}) collective-permute-start(bf16[2048,128]{1,0:T(8,128)(2,1)S(1)} %bitcast.17), channel_id=1, source_target_pairs={{0,96},{16,112},{32,0},{48,16},{64,32},{80,48},{96,64},{112,80},{1... | collective-permute-start | bytes 1572872 | tf_op jit(solution)/shard_map/ppermute | solution.py:190
  98.4 52.0 %collective-permute-start.1 = (bf16[2048,128]{1,0:T(8,128)(2,1)S(1)}, bf16[2048,128]{1,0:T(8,128)(2,1)}, u32[]{:S(2)}, u32[]{:S(2)}) collective-permute-start(bf16[2048,128]{1,0:T(8,128)(2,1)S(1)} %bitcast.18), channel_id=1, source_target_pairs={{0,16},{16,0},{32,48},{48,32},{64,80},{80,64},{96,112},{112,96},{1... | collective-permute-start | bytes 1572872 | tf_op jit(solution)/shard_map/ppermute | solution.py:191
  117.4 33.2 %collective-permute-start.11 = (bf16[2048,128]{1,0:T(8,128)(2,1)}, bf16[2048,128]{1,0:T(8,128)(2,1)}, u32[]{:S(2)}, u32[]{:S(2)}) collective-permute-start(bf16[2048,128]{1,0:T(8,128)(2,1)} %collective-permute-done.10.refs_10_), channel_id=1, source_target_pairs={{0,16},{16,0},{32,48},{48,32},{64,80},{80,64},{96,112},{112,96},{1... | collective-permute-start | bytes 1572872 | tf_op jit(solution)/shard_map/ppermute | solution.py:191
  117.5 33.4 %collective-permute-start.13 = (bf16[2048,128]{1,0:T(8,128)(2,1)}, bf16[2048,128]{1,0:T(8,128)(2,1)}, u32[]{:S(2)}, u32[]{:S(2)}) collective-permute-start(bf16[2048,128]{1,0:T(8,128)(2,1)} %collective-permute-done.12.refs_12_), channel_id=1, source_target_pairs={{0,16},{16,0},{32,48},{48,32},{64,80},{80,64},{96,112},{112,96},{1... | collective-permute-start | bytes 1572872 | tf_op jit(solution)/shard_map/ppermute | solution.py:191
  138.1 28.8 %all-to-all-start.2 = ((bf16[16,128,128]{2,1,0:T(8,128)(2,1)}), bf16[16,128,128]{2,1,0:T(8,128)(2,1)S(1)}, u32[]{:S(2)}, u32[]{:S(2)}) async-start(bf16[16,128,128]{2,1,0:T(8,128)(2,1)} %attend.1), calls=%async_computation.2 | async-start | bytes 1048576 | tf_op jit(solution)/shard_map/all_to_all | solution.py:198
  149.8 2.2 %collective-permute-start.15 = (bf16[2048,128]{1,0:T(8,128)(2,1)}, bf16[2048,128]{1,0:T(8,128)(2,1)S(1)}, u32[]{:S(2)}, u32[]{:S(2)}) collective-permute-start(bf16[2048,128]{1,0:T(8,128)(2,1)} %collective-permute-done.14.refs_14_), channel_id=1, source_target_pairs={{0,16},{16,0},{32,48},{48,32},{64,80},{80,64},{96,112},{112,96},{1... | collective-permute-start | bytes 1572872 | tf_op jit(solution)/shard_map/ppermute | solution.py:191
  149.9 2.8 %collective-permute-start.3 = (bf16[2048,128]{1,0:T(8,128)(2,1)}, bf16[2048,128]{1,0:T(8,128)(2,1)S(1)}, u32[]{:S(2)}, u32[]{:S(2)}) collective-permute-start(bf16[2048,128]{1,0:T(8,128)(2,1)} %collective-permute-done.2.refs_2_), channel_id=1, source_target_pairs={{0,16},{16,0},{32,48},{48,32},{64,80},{80,64},{96,112},{112,96},{1... | collective-permute-start | bytes 1572872 | tf_op jit(solution)/shard_map/ppermute | solution.py:191
  150.4 3.1 %collective-permute-start.5 = (bf16[2048,128]{1,0:T(8,128)(2,1)}, bf16[2048,128]{1,0:T(8,128)(2,1)S(1)}, u32[]{:S(2)}, u32[]{:S(2)}) collective-permute-start(bf16[2048,128]{1,0:T(8,128)(2,1)} %collective-permute-done.4.refs_4_), channel_id=1, source_target_pairs={{0,16},{16,0},{32,48},{48,32},{64,80},{80,64},{96,112},{112,96},{1... | collective-permute-start | bytes 1572872 | tf_op jit(solution)/shard_map/ppermute | solution.py:191
  150.7 3.6 %collective-permute-start.7 = (bf16[2048,128]{1,0:T(8,128)(2,1)}, bf16[2048,128]{1,0:T(8,128)(2,1)S(1)}, u32[]{:S(2)}, u32[]{:S(2)}) collective-permute-start(bf16[2048,128]{1,0:T(8,128)(2,1)} %collective-permute-done.6.refs_6_), channel_id=1, source_target_pairs={{0,16},{16,0},{32,48},{48,32},{64,80},{80,64},{96,112},{112,96},{1... | collective-permute-start | bytes 1572872 | tf_op jit(solution)/shard_map/ppermute | solution.py:191
  150.9 4.2 %collective-permute-start.9 = (bf16[2048,128]{1,0:T(8,128)(2,1)}, bf16[2048,128]{1,0:T(8,128)(2,1)}, u32[]{:S(2)}, u32[]{:S(2)}) collective-permute-start(bf16[2048,128]{1,0:T(8,128)(2,1)} %collective-permute-done.8.refs_8_), channel_id=1, source_target_pairs={{0,16},{16,0},{32,48},{48,32},{64,80},{80,64},{96,112},{112,96},{1... | collective-permute-start | bytes 1572872 | tf_op jit(solution)/shard_map/ppermute | solution.py:191
  152.0 14.9 %copy-start.3 = (bf16[2048,128]{1,0:T(8,128)(2,1)}, bf16[2048,128]{1,0:T(8,128)(2,1)S(1)}, u32[]{:S(2)}) copy-start(bf16[2048,128]{1,0:T(8,128)(2,1)S(1)} %collective-permute-done.15.refs_15_) | copy-start | bytes 1572868
  152.7 14.2 %copy-start.4 = (bf16[2048,128]{1,0:T(8,128)(2,1)}, bf16[2048,128]{1,0:T(8,128)(2,1)S(1)}, u32[]{:S(2)}) copy-start(bf16[2048,128]{1,0:T(8,128)(2,1)S(1)} %collective-permute-done.3.refs_3_) | copy-start | bytes 1572868
  153.5 13.4 %copy-start.5 = (bf16[2048,128]{1,0:T(8,128)(2,1)}, bf16[2048,128]{1,0:T(8,128)(2,1)S(1)}, u32[]{:S(2)}) copy-start(bf16[2048,128]{1,0:T(8,128)(2,1)S(1)} %collective-permute-done.5.refs_5_) | copy-start | bytes 1572868
  154.2 12.7 %copy-start.6 = (bf16[2048,128]{1,0:T(8,128)(2,1)}, bf16[2048,128]{1,0:T(8,128)(2,1)S(1)}, u32[]{:S(2)}) copy-start(bf16[2048,128]{1,0:T(8,128)(2,1)S(1)} %collective-permute-done.7.refs_7_) | copy-start | bytes 1572868
  166.9 0.8 copy-start.2

commit v2 on v1

--- a/solution.py
+++ b/solution.py
@@ -8,16 +8,18 @@
 from jax.experimental.pallas import tpu as pltpu
 from jax.sharding import PartitionSpec as P
 
+
 HEAD_DIM = 64
 LANES = 128
 TILE = 256
 
 
-def attend_kernel(low_ref, q_ref, own_ref, prev_ref, o_ref, kbuf, vbuf, s_ref, sem):
-    t = pl.program_id(0)
+def attend_kernel(low_ref, q_ref, own_ref, prev_ref, *refs, first):
+    o_ref, kbuf, vbuf, s_ref, sem = refs[-5:]
+    t = pl.program_id(0) + first
     groups = own_ref.shape[0]
 
-    @pl.when(t == 0)
+    @pl.when(pl.program_id(0) == 0)
     def _():
         copies = []
         for j, buf in enumerate((kbuf, vbuf)):
@@ -76,38 +78,40 @@
     o_ref[...] = out.astype(jnp.bfloat16).reshape(o_ref.shape)
 
 
-def attention(low, query, own, prev):
+def attention(low, query, own, prev, first, tiles, done):
     groups, rows, _ = query.shape
     per_tile = TILE // rows
-    tiles = groups // per_tile
     window = groups * rows + TILE
+    past = [] if done is None else [done]
     return pl.pallas_call(
-        attend_kernel,
+        functools.partial(attend_kernel, first=first),
         grid=(tiles,),
         out_shape=jax.ShapeDtypeStruct((groups, rows, LANES), jnp.bfloat16),
         in_specs=[
-            pl.BlockSpec((TILE, LANES), lambda t: (t, 0)),
-            pl.BlockSpec((per_tile, rows, LANES), lambda t: (t, 0, 0)),
+            pl.BlockSpec((TILE, LANES), lambda t: (t + first, 0)),
+            pl.BlockSpec((per_tile, rows, LANES), lambda t: (t + first, 0, 0)),
             pl.BlockSpec(memory_space=pl.ANY),
             pl.BlockSpec(memory_space=pl.ANY),
-        ],
-        out_specs=pl.BlockSpec((per_tile, rows, LANES), lambda t: (t, 0, 0)),
+        ]
+        + [pl.BlockSpec(memory_space=pl.ANY)] * len(past),
+        out_specs=pl.BlockSpec((per_tile, rows, LANES), lambda t: (t + first, 0, 0)),
         scratch_shapes=[
             pltpu.VMEM((2 * groups, rows, LANES), jnp.bfloat16),
             pltpu.VMEM((2 * groups, rows, LANES), jnp.bfloat16),
-            pltpu.VMEM((2, tiles + 1, TILE, TILE), jnp.float32),
+            pltpu.VMEM((2, window // TILE, TILE, TILE), jnp.float32),
             pltpu.SemaphoreType.DMA((4,)),
         ],
         compiler_params=pltpu.CompilerParams(
             dimension_semantics=("arbitrary",), vmem_limit_bytes=32 << 20
         ),
         cost_estimate=pl.CostEstimate(
-            flops=8 * groups * rows * window * LANES,
+            flops=8 * tiles * TILE * window * LANES,
             bytes_accessed=6 * groups * rows * LANES * 2,
-            transcendentals=2 * groups * rows * window,
-        ),
+            transcendentals=2 * tiles * TILE * window,
+        ),
+        input_output_aliases={4: 0} if past else {},
         name="attend",
-    )(low, query, own, prev)
+    )(low, query, own, prev, *past)
 
 
 def project_kernel(ctx_ref, *refs, shifts):
@@ -145,7 +149,7 @@
             pltpu.VMEM((len(pieces), depth, LANES), jnp.bfloat16),
             pltpu.SemaphoreType.DMA((len(pieces),)),
         ],
-        compiler_params=pltpu.CompilerParams(vmem_limit_bytes=60 << 20),
+        compiler_params=pltpu.CompilerParams(vmem_limit_bytes=50 << 20),
         cost_estimate=pl.CostEstimate(
             flops=2 * rows * depth * width, bytes_accessed=2 * depth * width, transcendentals=0
         ),
@@ -177,24 +181,33 @@
         tiled=True,
     )
     prev = lax.ppermute(kvw[:, :2], "blk", [(i, i + 1) for i in range(blks - 1)])
-    query = lax.all_to_all(split(queries), "head", 0, 0, tiled=True)
-
-    mine = kvw[:, 2].reshape(heads * w_out.shape[0], LANES)
+    query = split(queries)
+    query = lax.all_to_all(query, "head", 0, 0, tiled=True)
+
+    def shift(x, dx, dy):
+        pairs = []
+        for i in range(blks):
+            x0, y0, core = i // 8, (i // 2) % 4, i % 2
+            pairs.append((i, (x0 ^ dx) * 8 + ((y0 + dy) % 4) * 2 + core))
+        return lax.ppermute(x, "blk", pairs)
+
+    found = {(0, 0): kvw[:, 2].reshape(heads * w_out.shape[0], LANES)}
+    for dx, dy in ((0, 1), (1, 3), (1, 1), (0, 3), (1, 0)):
+        found[dx, dy] = shift(found[0, 0], dx, dy)
+    for dx, dy in ((0, 1), (1, 3)):
+        found[dx, 2] = shift(found[dx, dy], 0, dy)
     shifts = [(dx, dy) for dy in (0, 1, 3, 2) for dx in (0, 1)]
     pieces = []
-    for dx, dy in shifts:
-        pairs = []
-        for i in range(blks):
-            x, y, core = i // 8, (i // 2) % 4, i % 2
-            pairs.append((i, (x ^ dx) * 8 + ((y + dy) % 4) * 2 + core))
-        piece = mine if dx == dy == 0 else lax.ppermute(mine, "blk", pairs)
-        other = lax.ppermute(piece, "blk", [(i, i ^ 1) for i in range(blks)])
-        pieces += [piece, other]
+    for at in shifts:
+        other = lax.ppermute(found[at], "blk", [(i, i ^ 1) for i in range(blks)])
+        pieces += [found[at], other]
 
     tile_start = (jnp.arange(span, dtype=jnp.int32) // TILE) * TILE
     low = first_key - (place * span - span) - tile_start
     low = jnp.broadcast_to(low[:, None], (span, LANES))
-    ctx = attention(low, query, kvw, prev)
+    tiles = span // TILE
+    ctx = attention(low, query, kvw, prev, 0, tiles // 2, None)
+    ctx = attention(low, query, kvw, prev, tiles // 2, tiles - tiles // 2, ctx)
     ctx = lax.all_to_all(ctx, "head", 0, 0, tiled=True)
     return project(ctx, pieces, shifts)
 

time: 175 us -> 152 us (0.87)
  the two profiles are of different devices: /device:TPU:2 before, /device:TPU:1 now
where the time goes in v2:
time: 152 us; the launch traced here: 151 us
  blocking collectives  49.1 us (32%)
  starting transfers between devices  34 us (22%)
  waiting for transfers between devices  33.3 us (22%)
  Pallas kernels  27.5 us (18%)
  local copies, waits for them, and re-layouts  6.67 us (4%)
    all_to_all x1, blocking collectives, layer(): lax.all_to_all(jnp.stack([split(key_rows), split(value_rows), jnp.broadca...  49.1 us
    pallas_call x2, Pallas kernels, attention(): pl.pallas_call(functools.partial(attend_kernel, first=first), grid=(tiles...  22.1 us
    ppermute x7, waiting for transfers between devices, shift(): return lax.ppermute(x, 'blk', pairs)  11.3 us
    ppermute x7, starting transfers between devices, shift(): return lax.ppermute(x, 'blk', pairs)  11.1 us
    all_to_all x1, waiting for transfers between devices, layer(): ctx = lax.all_to_all(ctx, 'head', 0, 0, tiled=True)  10.6 us
    all_to_all x1, starting transfers between devices, layer(): ctx = lax.all_to_all(ctx, 'head', 0, 0, tiled=True)  8.62 us
    ppermute x1, waiting for transfers between devices, layer(): lax.ppermute(kvw[:, :2], 'blk', [(i, i + 1) for i in range(blks - 1)])  7.04 us
    ppermute x1, starting transfers between devices, layer(): lax.ppermute(kvw[:, :2], 'blk', [(i, i + 1) for i in range(blks - 1)])  5.92 us
  transfers between devices with their start and end apart: 18, of which 9 were waited for; matrix products, arithmetic and copies ran while one was open for 1% of the time, Pallas kernels for 15%

profile of v2, /device:TPU:1, one launch (start us, length us, event | category | flops | bytes accessed | tf_op | source)
XLA Modules:
  0.0 151.2 jit_solution(11117948076767621867)
XLA Ops:
  0.0 1.4 copy.9
  2.6 49.1 %all_to_all.15.own_ref = bf16[16,3,128,128]{3,2,1,0:T(8,128)(2,1)S(1)} all-to-all(bf16[16,3,128,128]{3,2,1,0:T(8,128)(2,1)S(1)} %pad_maximum_fusion), channel_id=1, replica_groups=mesh['blk'=16,'head'=16] {'head'}, dimensions={0} | all-to-all | bytes 3145728 | tf_op jit(solution)/shard_map/all_to_all | solution.py:169
  51.7 1.0 slice.8
  52.7 5.9 %collective-permute-start = (bf16[16,2,128,128]{3,2,1,0:T(8,128)(2,1)}, bf16[16,2,128,128]{3,2,1,0:T(8,128)(2,1)}, u32[]{:S(2)}, u32[]{:S(2)}) collective-permute-start(bf16[16,2,128,128]{3,2,1,0:T(8,128)(2,1)} %slice.8), channel_id=1, source_target_pairs={{0,16},{16,32},{32,48},{48,64},{64,80},{80,96},{96,112},{112,128},... | collective-permute-start | bytes 3145736 | tf_op jit(solution)/shard_map/ppermute | solution.py:183
  59.0 1.0 copy.8
  60.0 4.4 %all-to-all-start = ((bf16[16,128,128]{2,1,0:T(8,128)(2,1)}), bf16[16,128,128]{2,1,0:T(8,128)(2,1)}, u32[]{:S(2)}, u32[]{:S(2)}) async-start(bf16[16,128,128]{2,1,0:T(8,128)(2,1)} %bitcast.1), calls=%async_computation | async-start | bytes 1048576 | tf_op jit(solution)/shard_map/all_to_all | solution.py:185
  64.4 1.4 collective-permute-start.4
  65.7 1.4 collective-permute-start.10
  67.1 1.2 collective-permute-start.2
  68.4 7.0 %collective-permute-done.prev_ref = bf16[16,2,128,128]{3,2,1,0:T(8,128)(2,1)} collective-permute-done((bf16[16,2,128,128]{3,2,1,0:T(8,128)(2,1)}, bf16[16,2,128,128]{3,2,1,0:T(8,128)(2,1)}, u32[]{:S(2)}, u32[]{:S(2)}) %collective-permute-start) | collective-permute-done | bytes 1048608 | tf_op jit(solution)/shard_map/ppermute | solution.py:183
  75.5 5.1 %collective-permute-start.8 = (bf16[2048,128]{1,0:T(8,128)(2,1)S(1)}, bf16[2048,128]{1,0:T(8,128)(2,1)}, u32[]{:S(2)}, u32[]{:S(2)}) collective-permute-start(bf16[2048,128]{1,0:T(8,128)(2,1)S(1)} %bitcast.15), channel_id=1, source_target_pairs={{0,96},{16,112},{32,0},{48,16},{64,32},{80,48},{96,64},{112,80},{1... | collective-permute-start | bytes 1572872 | tf_op jit(solution)/shard_map/ppermute | solution.py:192
  80.6 1.3 all-to-all-done.q_ref
  81.9 0.3 broadcast_in_dim.2.low_ref
  82.2 11.0 %attend.2.refs_0_ = bf16[16,128,128]{2,1,0:T(8,128)(2,1)S(1)} custom-call(s32[2048,128]{1,0:T(8,128)S(1)} %broadcast_in_dim.2.low_ref, bf16[16,128,128]{2,1,0:T(8,128)(2,1)} %all-to-all-done.q_ref, bf16[16,3,128,128]{3,2,1,0:T(8,128)(2,1)S(1)} %all_to_all.15.own_ref, bf16[16,2,128,128]{3,2,1,0:T(8,128)(2,1)} %collective-permute-done.prev_ref), custom_call_target="tpu_custom_call" | custom-call | flops 2415919104 | bytes 3145728 | tf_op jit(solution)/shard_map/attend/pallas_call | solution.py:86
  93.3 0.6 collective-permute-start.1
  93.9 1.8 %collective-permute-start.14 = (bf16[2048,128]{1,0:T(8,128)(2,1)}, bf16[2048,128]{1,0:T(8,128)(2,1)}, u32[]{:S(2)}, u32[]{:S(2)}) collective-permute-start(bf16[2048,128]{1,0:T(8,128)(2,1)} %collective-permute-done.10.refs_10_), channel_id=1, source_target_pairs={{0,96},{16,112},{32,0},{48,16},{64,32},{80,48},{96,64},{112,80},{1... | collective-permute-start | bytes 1572872 | tf_op jit(solution)/shard_map/ppermute | solution.py:192
  95.8 1.0 collective-permute-start.11
  96.8 11.2 %collective-permute-done.6.refs_6_ = bf16[2048,128]{1,0:T(8,128)(2,1)} collective-permute-done((bf16[2048,128]{1,0:T(8,128)(2,1)S(1)}, bf16[2048,128]{1,0:T(8,128)(2,1)}, u32[]{:S(2)}, u32[]{:S(2)}) %collective-permute-start.6) | collective-permute-done | bytes 524320 | tf_op jit(solution)/shard_map/ppermute | solution.py:192
  108.2 1.0 collective-permute-start.5
  109.2 11.0 %attend.3 = bf16[16,128,128]{2,1,0:T(8,128)(2,1)S(1)} custom-call(s32[2048,128]{1,0:T(8,128)S(1)} %broadcast_in_dim.2.low_ref, bf16[16,128,128]{2,1,0:T(8,128)(2,1)} %all-to-all-done.q_ref, bf16[16,3,128,128]{3,2,1,0:T(8,128)(2,1)S(1)} %all_to_all.15.own_ref, ...), custom_call_target="tpu_custom_call", output_to_operand_aliasing={{}: (4, {})} | custom-call | flops 2415919104 | bytes 3145728 | tf_op jit(solution)/shard_map/attend/pallas_call | solution.py:86
  120.3 0.8 copy-done.1
  121.0 8.6 %all-to-all-start.2 = ((bf16[16,128,128]{2,1,0:T(8,128)(2,1)}), bf16[16,128,128]{2,1,0:T(8,128)(2,1)S(1)}, u32[]{:S(2)}, u32[]{:S(2)}) async-start(bf16[16,128,128]{2,1,0:T(8,128)(2,1)} %copy-done.1), calls=%async_computation.2 | async-start | bytes 1048576 | tf_op jit(solution)/shard_map/all_to_all | solution.py:211
  129.7 0.4 collective-permute-start.3
  130.3 0.3 collective-permute-start.9
  130.8 0.3 collective-permute-start.15
  131.1 0.8 collective-permute-done.3.refs_3_
  131.9 0.7 collective-permute-done.7.refs_7_
  132.6 0.7 collective-permute-done.9.refs_9_
  133.4 0.7 collective-permute-done.13.refs_13_
  134.2 0.8 copy-done.4
  135.0 10.6 %all-to-all-done.2.ctx_ref = bf16[16,128,128]{2,1,0:T(8,128)(2,1)S(1)} async-done(((bf16[16,128,128]{2,1,0:T(8,128)(2,1)}), bf16[16,128,128]{2,1,0:T(8,128)(2,1)S(1)}, u32[]{:S(2)}, u32[]{:S(2)}) %all-to-all-start.2) | async-done | bytes 524320 | tf_op jit(solution)/shard_map/all_to_all | solution.py:211
  145.6 5.4 %project.1 = bf16[128,2048]{1,0:T(8,128)(2,1)} custom-call(bf16[16,128,128]{2,1,0:T(8,128)(2,1)S(1)} %all-to-all-done.2.ctx_ref, bf16[2048,128]{1,0:T(8,128)(2,1)S(1)} %bitcast.17, bf16[2048,128]{1,0:T(8,128)(2,1)} %collective-permute-done.1.refs_1_, bf16[2048,128]{1,0:T(8,128)(2,1)} %collective-permute-done.2.refs_2_, ...), custom_call_target="tpu_custom_call" | custom-call | flops 1073741824 | bytes 8388608 | tf_op jit(solution)/shard_map/project/pallas_call | solution.py:142
  (37 shorter events, 2.3 us)
Async XLA Ops:
  0.0 2.3 %copy-start = (bf16[128,2048]{1,0:T(8,128)(2,1)S(1)}, bf16[128,2048]{1,0:T(8,128)(2,1)}, u32[]{:S(2)}) copy-start(bf16[128,2048]{1,0:T(8,128)(2,1)} %param.8) | copy-start | bytes 1572868
  0.0 1.7 %copy-start.5 = (bf16[128,2048]{1,0:T(8,128)(2,1)S(1)}, bf16[128,2048]{1,0:T(8,128)(2,1)}, u32[]{:S(2)}) copy-start(bf16[128,2048]{1,0:T(8,128)(2,1)} %param.7) | copy-start | bytes 1572868
  51.7 7.0 %copy-start.6 = (bf16[128,2048]{1,0:T(8,128)(2,1)S(1)}, bf16[128,2048]{1,0:T(8,128)(2,1)}, u32[]{:S(2)}) copy-start(bf16[128,2048]{1,0:T(8,128)(2,1)} %param.5) | copy-start | bytes 1572868
  52.7 22.7 %collective-permute-start = (bf16[16,2,128,128]{3,2,1,0:T(8,128)(2,1)}, bf16[16,2,128,128]{3,2,1,0:T(8,128)(2,1)}, u32[]{:S(2)}, u32[]{:S(2)}) collective-permute-start(bf16[16,2,128,128]{3,2,1,0:T(8,128)(2,1)} %slice.8), channel_id=1, source_target_pairs={{0,16},{16,32},{32,48},{48,64},{64,80},{80,96},{96,112},{112,128},... | collective-permute-start | bytes 3145736 | tf_op jit(solution)/shard_map/ppermute | solution.py:183
  58.9 21.6 %copy-start.7 = (s32[2048]{0:T(1024)S(1)}, s32[2048]{0:T(1024)}, u32[]{:S(2)}) copy-start(s32[2048]{0:T(1024)} %param.9) | copy-start | bytes 24580
  60.0 21.9 %all-to-all-start = ((bf16[16,128,128]{2,1,0:T(8,128)(2,1)}), bf16[16,128,128]{2,1,0:T(8,128)(2,1)}, u32[]{:S(2)}, u32[]{:S(2)}) async-start(bf16[16,128,128]{2,1,0:T(8,128)(2,1)} %bitcast.1), calls=%async_computation | async-start | bytes 1048576 | tf_op jit(solution)/shard_map/all_to_all | solution.py:185
  64.4 28.9 %collective-permute-start.4 = (bf16[2048,128]{1,0:T(8,128)(2,1)S(1)}, bf16[2048,128]{1,0:T(8,128)(2,1)S(1)}, u32[]{:S(2)}, u32[]{:S(2)}) collective-permute-start(bf16[2048,128]{1,0:T(8,128)(2,1)S(1)} %bitcast.11), channel_id=1, source_target_pairs={{0,32},{16,48},{32,64},{48,80},{64,96},{80,112},{96,0},{112,16},{1... | collective-permute-start | bytes 1572872 | tf_op jit(solution)/shard_map/ppermute | solution.py:192
  65.7 28.2 %collective-permute-start.10 = (bf16[2048,128]{1,0:T(8,128)(2,1)S(1)}, bf16[2048,128]{1,0:T(8,128)(2,1)}, u32[]{:S(2)}, u32[]{:S(2)}) collective-permute-start(bf16[2048,128]{1,0:T(8,128)(2,1)S(1)} %bitcast.12), channel_id=1, source_target_pairs={{0,224},{16,240},{32,128},{48,144},{64,160},{80,176},{96,192},{112... | collective-permute-start | bytes 1572872 | tf_op jit(solution)/shard_map/ppermute | solution.py:192
  67.1 28.6 %collective-permute-start.2 = (bf16[2048,128]{1,0:T(8,128)(2,1)S(1)}, bf16[2048,128]{1,0:T(8,128)(2,1)}, u32[]{:S(2)}, u32[]{:S(2)}) collective-permute-start(bf16[2048,128]{1,0:T(8,128)(2,1)S(1)} %bitcast.13), channel_id=1, source_target_pairs={{0,128},{16,144},{32,160},{48,176},{64,192},{80,208},{96,224},{112... | collective-permute-start | bytes 1572872 | tf_op jit(solution)/shard_map/ppermute | solution.py:192
  68.3 39.7 %collective-permute-start.6 = (bf16[2048,128]{1,0:T(8,128)(2,1)S(1)}, bf16[2048,128]{1,0:T(8,128)(2,1)}, u32[]{:S(2)}, u32[]{:S(2)}) collective-permute-start(bf16[2048,128]{1,0:T(8,128)(2,1)S(1)} %bitcast.14), channel_id=1, source_target_pairs={{0,160},{16,176},{32,192},{48,208},{64,224},{80,240},{96,128},{112... | collective-permute-start | bytes 1572872 | tf_op jit(solution)/shard_map/ppermute | solution.py:192
  75.5 32.7 %collective-permute-start.8 = (bf16[2048,128]{1,0:T(8,128)(2,1)S(1)}, bf16[2048,128]{1,0:T(8,128)(2,1)}, u32[]{:S(2)}, u32[]{:S(2)}) collective-permute-start(bf16[2048,128]{1,0:T(8,128)(2,1)S(1)} %bitcast.15), channel_id=1, source_target_pairs={{0,96},{16,112},{32,0},{48,16},{64,32},{80,48},{96,64},{112,80},{1... | collective-permute-start | bytes 1572872 | tf_op jit(solution)/shard_map/ppermute | solution.py:192
  93.3 36.4 %collective-permute-start.1 = (bf16[2048,128]{1,0:T(8,128)(2,1)S(1)}, bf16[2048,128]{1,0:T(8,128)(2,1)}, u32[]{:S(2)}, u32[]{:S(2)}) collective-permute-start(bf16[2048,128]{1,0:T(8,128)(2,1)S(1)} %bitcast.16), channel_id=1, source_target_pairs={{0,16},{16,0},{32,48},{48,32},{64,80},{80,64},{96,112},{112,96},{1... | collective-permute-start | bytes 1572872 | tf_op jit(solution)/shard_map/ppermute | solution.py:202
  93.9 36.4 %collective-permute-start.14 = (bf16[2048,128]{1,0:T(8,128)(2,1)}, bf16[2048,128]{1,0:T(8,128)(2,1)}, u32[]{:S(2)}, u32[]{:S(2)}) collective-permute-start(bf16[2048,128]{1,0:T(8,128)(2,1)} %collective-permute-done.10.refs_10_), channel_id=1, source_target_pairs={{0,96},{16,112},{32,0},{48,16},{64,32},{80,48},{96,64},{112,80},{1... | collective-permute-start | bytes 1572872 | tf_op jit(solution)/shard_map/ppermute | solution.py:192
  95.8 34.8 %collective-permute-start.11 = (bf16[2048,128]{1,0:T(8,128)(2,1)}, bf16[2048,128]{1,0:T(8,128)(2,1)}, u32[]{:S(2)}, u32[]{:S(2)}) collective-permute-start(bf16[2048,128]{1,0:T(8,128)(2,1)} %collective-permute-done.10.refs_10_), channel_id=1, source_target_pairs={{0,16},{16,0},{32,48},{48,32},{64,80},{80,64},{96,112},{112,96},{1... | collective-permute-start | bytes 1572872 | tf_op jit(solution)/shard_map/ppermute | solution.py:202
  108.0 22.0 %collective-permute-start.12 = (bf16[2048,128]{1,0:T(8,128)(2,1)S(1)}, bf16[2048,128]{1,0:T(8,128)(2,1)}, u32[]{:S(2)}, u32[]{:S(2)}) collective-permute-start(bf16[2048,128]{1,0:T(8,128)(2,1)S(1)} %collective-permute-done.4.refs_4_), channel_id=1, source_target_pairs={{0,32},{16,48},{32,64},{48,80},{64,96},{80,112},{96,0},{112,16},{1... | collective-permute-start | bytes 1572872 | tf_op jit(solution)/shard_map/ppermute | solution.py:192
  108.2 22.6 %collective-permute-start.5 = (bf16[2048,128]{1,0:T(8,128)(2,1)S(1)}, bf16[2048,128]{1,0:T(8,128)(2,1)}, u32[]{:S(2)}, u32[]{:S(2)}) collective-permute-start(bf16[2048,128]{1,0:T(8,128)(2,1)S(1)} %collective-permute-done.4.refs_4_), channel_id=1, source_target_pairs={{0,16},{16,0},{32,48},{48,32},{64,80},{80,64},{96,112},{112,96},{1... | collective-permute-start | bytes 1572872 | tf_op jit(solution)/shard_map/ppermute | solution.py:202
  120.2 0.8 copy-start.1
  121.0 24.5 %all-to-all-start.2 = ((bf16[16,128,128]{2,1,0:T(8,128)(2,1)}), bf16[16,128,128]{2,1,0:T(8,128)(2,1)S(1)}, u32[]{:S(2)}, u32[]{:S(2)}) async-start(bf16[16,128,128]{2,1,0:T(8,128)(2,1)} %copy-done.1), calls=%async_computation.2 | async-start | bytes 1048576 | tf_op jit(solution)/shard_map/all_to_all | solution.py:211
  129.7 2.2 %collective-permute-start.3 = (bf16[2048,128]{1,0:T(8,128)(2,1)}, bf16[2048,128]{1,0:T(8,128)(2,1)S(1)}, u32[]{:S(2)}, u32[]{:S(2)}) collective-permute-start(bf16[2048,128]{1,0:T(8,128)(2,1)} %collective-permute-done.2.refs_2_), channel_id=1, source_target_pairs={{0,16},{16,0},{32,48},{48,32},{64,80},{80,64},{96,112},{112,96},{1... | collective-permute-start | bytes 1572872 | tf_op jit(solution)/shard_map/ppermute | solution.py:202
  130.0 2.6 %collective-permute-start.7 = (bf16[2048,128]{1,0:T(8,128)(2,1)}, bf16[2048,128]{1,0:T(8,128)(2,1)S(1)}, u32[]{:S(2)}, u32[]{:S(2)}) collective-permute-start(bf16[2048,128]{1,0:T(8,128)(2,1)} %collective-permute-done.6.refs_6_), channel_id=1, source_target_pairs={{0,16},{16,0},{32,48},{48,32},{64,80},{80,64},{96,112},{112,96},{1... | collective-permute-start | bytes 1572872 | tf_op jit(solution)/shard_map/ppermute | solution.py:202
  130.3 3.1 %collective-permute-start.9 = (bf16[2048,128]{1,0:T(8,128)(2,1)}, bf16[2048,128]{1,0:T(8,128)(2,1)S(1)}, u32[]{:S(2)}, u32[]{:S(2)}) collective-permute-start(bf16[2048,128]{1,0:T(8,128)(2,1)} %collective-permute-done.8.refs_8_), channel_id=1, source_target_pairs={{0,16},{16,0},{32,48},{48,32},{64,80},{80,64},{96,112},{112,96},{1... | collective-permute-start | bytes 1572872 | tf_op jit(solution)/shard_map/ppermute | solution.py:202
  130.6 3.6 %collective-permute-start.13 = (bf16[2048,128]{1,0:T(8,128)(2,1)}, bf16[2048,128]{1,0:T(8,128)(2,1)S(1)}, u32[]{:S(2)}, u32[]{:S(2)}) collective-permute-start(bf16[2048,128]{1,0:T(8,128)(2,1)} %collective-permute-done.12.refs_12_), channel_id=1, source_target_pairs={{0,16},{16,0},{32,48},{48,32},{64,80},{80,64},{96,112},{112,96},{1... | collective-permute-start | bytes 1572872 | tf_op jit(solution)/shard_map/ppermute | solution.py:202
  130.8 4.2 %collective-permute-start.15 = (bf16[2048,128]{1,0:T(8,128)(2,1)}, bf16[2048,128]{1,0:T(8,128)(2,1)}, u32[]{:S(2)}, u32[]{:S(2)}) collective-permute-start(bf16[2048,128]{1,0:T(8,128)(2,1)} %collective-permute-done.14.refs_14_), channel_id=1, source_target_pairs={{0,16},{16,0},{32,48},{48,32},{64,80},{80,64},{96,112},{112,96},{1... | collective-permute-start | bytes 1572872 | tf_op jit(solution)/shard_map/ppermute | solution.py:202
  132.6 13.0 %copy-start.2 = (bf16[2048,128]{1,0:T(8,128)(2,1)}, bf16[2048,128]{1,0:T(8,128)(2,1)S(1)}, u32[]{:S(2)}) copy-start(bf16[2048,128]{1,0:T(8,128)(2,1)S(1)} %collective-permute-done.7.refs_7_) | copy-start | bytes 1572868
  133.4 0.8 copy-start.3
  134.2 0.8 copy-start.4

commit v3 on v1

--- a/solution.py
+++ b/solution.py
@@ -7,6 +7,7 @@
 from jax.experimental import pallas as pl
 from jax.experimental.pallas import tpu as pltpu
 from jax.sharding import PartitionSpec as P
+
 
 HEAD_DIM = 64
 LANES = 128
@@ -145,7 +146,7 @@
             pltpu.VMEM((len(pieces), depth, LANES), jnp.bfloat16),
             pltpu.SemaphoreType.DMA((len(pieces),)),
         ],
-        compiler_params=pltpu.CompilerParams(vmem_limit_bytes=60 << 20),
+        compiler_params=pltpu.CompilerParams(vmem_limit_bytes=50 << 20),
         cost_estimate=pl.CostEstimate(
             flops=2 * rows * depth * width, bytes_accessed=2 * depth * width, transcendentals=0
         ),
@@ -177,19 +178,26 @@
         tiled=True,
     )
     prev = lax.ppermute(kvw[:, :2], "blk", [(i, i + 1) for i in range(blks - 1)])
-    query = lax.all_to_all(split(queries), "head", 0, 0, tiled=True)
-
-    mine = kvw[:, 2].reshape(heads * w_out.shape[0], LANES)
+    query = split(queries)
+    query = lax.all_to_all(query, "head", 0, 0, tiled=True)
+
+    def shift(x, dx, dy):
+        pairs = []
+        for i in range(blks):
+            x0, y0, core = i // 8, (i // 2) % 4, i % 2
+            pairs.append((i, (x0 ^ dx) * 8 + ((y0 + dy) % 4) * 2 + core))
+        return lax.ppermute(x, "blk", pairs)
+
+    found = {(0, 0): kvw[:, 2].reshape(heads * w_out.shape[0], LANES)}
+    for dx, dy in ((0, 1), (1, 3), (1, 1), (0, 3), (1, 0)):
+        found[dx, dy] = shift(found[0, 0], dx, dy)
+    for dx, dy in ((0, 1), (1, 3)):
+        found[dx, 2] = shift(found[dx, dy], 0, dy)
     shifts = [(dx, dy) for dy in (0, 1, 3, 2) for dx in (0, 1)]
     pieces = []
-    for dx, dy in shifts:
-        pairs = []
-        for i in range(blks):
-            x, y, core = i // 8, (i // 2) % 4, i % 2
-            pairs.append((i, (x ^ dx) * 8 + ((y + dy) % 4) * 2 + core))
-        piece = mine if dx == dy == 0 else lax.ppermute(mine, "blk", pairs)
-        other = lax.ppermute(piece, "blk", [(i, i ^ 1) for i in range(blks)])
-        pieces += [piece, other]
+    for at in shifts:
+        other = lax.ppermute(found[at], "blk", [(i, i ^ 1) for i in range(blks)])
+        pieces += [found[at], other]
 
     tile_start = (jnp.arange(span, dtype=jnp.int32) // TILE) * TILE
     low = first_key - (place * span - span) - tile_start

time: 175 us -> 165 us (0.943)
  the two profiles are of different devices: /device:TPU:2 before, /device:TPU:1 now
where the time goes in v3:
time: 165 us; the launch traced here: 164 us
  blocking collectives  49.1 us (30%)
  waiting for transfers between devices  43.8 us (27%)
  starting transfers between devices  35.5 us (22%)
  Pallas kernels  25.4 us (15%)
  local copies, waits for them, and re-layouts  9.49 us (6%)
    all_to_all x1, blocking collectives, layer(): lax.all_to_all(jnp.stack([split(key_rows), split(value_rows), jnp.broadca...  49.1 us
    ppermute x7, waiting for transfers between devices, shift(): return lax.ppermute(x, 'blk', pairs)  30.3 us
    pallas_call x1, Pallas kernels, attention(): pl.pallas_call(attend_kernel, grid=(tiles,), out_shape=jax.ShapeDtypeStru...  20 us
    ppermute x7, starting transfers between devices, shift(): return lax.ppermute(x, 'blk', pairs)  13.2 us
    all_to_all x1, waiting for transfers between devices, layer(): ctx = lax.all_to_all(ctx, 'head', 0, 0, tiled=True)  10.4 us
    all_to_all x1, starting transfers between devices, layer(): ctx = lax.all_to_all(ctx, 'head', 0, 0, tiled=True)  8.27 us
    ppermute x1, starting transfers between devices, layer(): lax.ppermute(kvw[:, :2], 'blk', [(i, i + 1) for i in range(blks - 1)])  6.33 us
    pallas_call x1, Pallas kernels, project(): pl.pallas_call(functools.partial(project_kernel, shifts=shifts), out_shap...  5.43 us
  transfers between devices with their start and end apart: 18, of which 8 were waited for; matrix products, arithmetic and copies ran while one was open for 3% of the time, Pallas kernels for 12%

profile of v3, /device:TPU:1, one launch (start us, length us, event | category | flops | bytes accessed | tf_op | source)
XLA Modules:
  0.0 163.8 jit_solution(2721052221501610622)
XLA Ops:
  0.0 1.4 copy.8
  2.6 49.1 %all_to_all.15.own_ref = bf16[16,3,128,128]{3,2,1,0:T(8,128)(2,1)S(1)} all-to-all(bf16[16,3,128,128]{3,2,1,0:T(8,128)(2,1)S(1)} %pad_maximum_fusion), channel_id=1, replica_groups=mesh['blk'=16,'head'=16] {'head'}, dimensions={0} | all-to-all | bytes 3145728 | tf_op jit(solution)/shard_map/all_to_all | solution.py:166
  51.7 1.4 collective-permute-start.4
  53.1 1.0 slice.8
  54.2 6.3 %collective-permute-start = (bf16[16,2,128,128]{3,2,1,0:T(8,128)(2,1)}, bf16[16,2,128,128]{3,2,1,0:T(8,128)(2,1)}, u32[]{:S(2)}, u32[]{:S(2)}) collective-permute-start(bf16[16,2,128,128]{3,2,1,0:T(8,128)(2,1)} %slice.8), channel_id=1, source_target_pairs={{0,16},{16,32},{32,48},{48,64},{64,80},{80,96},{96,112},{112,128},... | collective-permute-start | bytes 3145736 | tf_op jit(solution)/shard_map/ppermute | solution.py:180
  60.5 2.0 %copy.6 = bf16[128,2048]{0,1:T(8,128)(2,1)} copy(bf16[128,2048]{1,0:T(8,128)(2,1)} %param.5) | data formatting | bytes 1048576 | tf_op args[0]
  62.5 2.0 %copy.7 = bf16[128,16,128]{2,0,1:T(8,128)(2,1)} copy(bf16[128,16,128]{0,2,1:T(8,128)(2,1)} %bitcast.21) | data formatting | bytes 1048576 | tf_op jit(solution)/shard_map/reshape | solution.py:163
  64.6 4.4 %all-to-all-start = ((bf16[16,128,128]{2,1,0:T(8,128)(2,1)}), bf16[16,128,128]{2,1,0:T(8,128)(2,1)}, u32[]{:S(2)}, u32[]{:S(2)}) async-start(bf16[16,128,128]{2,1,0:T(8,128)(2,1)} %bitcast.18), calls=%async_computation | async-start | bytes 1048576 | tf_op jit(solution)/shard_map/all_to_all | solution.py:182
  69.0 3.2 %collective-permute-start.2 = (bf16[2048,128]{1,0:T(8,128)(2,1)S(1)}, bf16[2048,128]{1,0:T(8,128)(2,1)}, u32[]{:S(2)}, u32[]{:S(2)}) collective-permute-start(bf16[2048,128]{1,0:T(8,128)(2,1)S(1)} %bitcast.13), channel_id=1, source_target_pairs={{0,128},{16,144},{32,160},{48,176},{64,192},{80,208},{96,224},{112... | collective-permute-start | bytes 1572872 | tf_op jit(solution)/shard_map/ppermute | solution.py:189
  72.2 2.4 %collective-permute-start.8 = (bf16[2048,128]{1,0:T(8,128)(2,1)S(1)}, bf16[2048,128]{1,0:T(8,128)(2,1)}, u32[]{:S(2)}, u32[]{:S(2)}) collective-permute-start(bf16[2048,128]{1,0:T(8,128)(2,1)S(1)} %bitcast.15), channel_id=1, source_target_pairs={{0,96},{16,112},{32,0},{48,16},{64,32},{80,48},{96,64},{112,80},{1... | collective-permute-start | bytes 1572872 | tf_op jit(solution)/shard_map/ppermute | solution.py:189
  74.6 14.2 %collective-permute-done.10.refs_10_ = bf16[2048,128]{1,0:T(8,128)(2,1)} collective-permute-done((bf16[2048,128]{1,0:T(8,128)(2,1)S(1)}, bf16[2048,128]{1,0:T(8,128)(2,1)}, u32[]{:S(2)}, u32[]{:S(2)}) %collective-permute-start.10) | collective-permute-done | bytes 524320 | tf_op jit(solution)/shard_map/ppermute | solution.py:189
  88.8 0.5 collective-permute-start.1
  89.3 10.4 %collective-permute-done.2.refs_2_ = bf16[2048,128]{1,0:T(8,128)(2,1)} collective-permute-done((bf16[2048,128]{1,0:T(8,128)(2,1)S(1)}, bf16[2048,128]{1,0:T(8,128)(2,1)}, u32[]{:S(2)}, u32[]{:S(2)}) %collective-permute-start.2) | collective-permute-done | bytes 524320 | tf_op jit(solution)/shard_map/ppermute | solution.py:189
  99.7 4.8 %collective-permute-start.14 = (bf16[2048,128]{1,0:T(8,128)(2,1)}, bf16[2048,128]{1,0:T(8,128)(2,1)}, u32[]{:S(2)}, u32[]{:S(2)}) collective-permute-start(bf16[2048,128]{1,0:T(8,128)(2,1)} %collective-permute-done.10.refs_10_), channel_id=1, source_target_pairs={{0,96},{16,112},{32,0},{48,16},{64,32},{80,48},{96,64},{112,80},{1... | collective-permute-start | bytes 1572872 | tf_op jit(solution)/shard_map/ppermute | solution.py:189
  104.5 5.7 %collective-permute-done.6.refs_6_ = bf16[2048,128]{1,0:T(8,128)(2,1)} collective-permute-done((bf16[2048,128]{1,0:T(8,128)(2,1)S(1)}, bf16[2048,128]{1,0:T(8,128)(2,1)}, u32[]{:S(2)}, u32[]{:S(2)}) %collective-permute-start.6) | collective-permute-done | bytes 524320 | tf_op jit(solution)/shard_map/ppermute | solution.py:189
  110.2 0.9 collective-permute-start.11
  111.1 1.3 collective-permute-start.12
  112.4 0.4 collective-permute-start.5
  112.8 0.3 broadcast_in_dim.2.low_ref
  113.2 20.0 %attend.1 = bf16[16,128,128]{2,1,0:T(8,128)(2,1)S(1)} custom-call(s32[2048,128]{1,0:T(8,128)S(1)} %broadcast_in_dim.2.low_ref, bf16[16,128,128]{2,1,0:T(8,128)(2,1)} %all-to-all-done.q_ref, bf16[16,3,128,128]{3,2,1,0:T(8,128)(2,1)S(1)} %all_to_all.15.own_ref, bf16[16,2,128,128]{3,2,1,0:T(8,128)(2,1)} %collective-permute-done.prev_ref), custom_call_target="tpu_custom_call" | custom-call | flops 4831838208 | bytes 3145728 | tf_op jit(solution)/shard_map/attend/pallas_call | solution.py:85
  133.2 0.8 copy-done.1
  134.0 8.3 %all-to-all-start.2 = ((bf16[16,128,128]{2,1,0:T(8,128)(2,1)}), bf16[16,128,128]{2,1,0:T(8,128)(2,1)S(1)}, u32[]{:S(2)}, u32[]{:S(2)}) async-start(bf16[16,128,128]{2,1,0:T(8,128)(2,1)} %copy-done.1), calls=%async_computation.2 | async-start | bytes 1048576 | tf_op jit(solution)/shard_map/all_to_all | solution.py:206
  142.3 0.6 collective-permute-start.3
  143.0 0.3 collective-permute-start.9
  143.6 0.3 collective-permute-start.15
  143.9 0.8 collective-permute-done.3.refs_3_
  144.6 0.7 collective-permute-done.7.refs_7_
  145.4 0.7 collective-permute-done.9.refs_9_
  146.2 0.7 collective-permute-done.13.refs_13_
  146.9 0.8 copy-done.4
  147.8 10.4 %all-to-all-done.2.ctx_ref = bf16[16,128,128]{2,1,0:T(8,128)(2,1)S(1)} async-done(((bf16[16,128,128]{2,1,0:T(8,128)(2,1)}), bf16[16,128,128]{2,1,0:T(8,128)(2,1)S(1)}, u32[]{:S(2)}, u32[]{:S(2)}) %all-to-all-start.2) | async-done | bytes 524320 | tf_op jit(solution)/shard_map/all_to_all | solution.py:206
  158.2 5.4 %project.1 = bf16[128,2048]{1,0:T(8,128)(2,1)} custom-call(bf16[16,128,128]{2,1,0:T(8,128)(2,1)S(1)} %all-to-all-done.2.ctx_ref, bf16[2048,128]{1,0:T(8,128)(2,1)S(1)} %bitcast.17, bf16[2048,128]{1,0:T(8,128)(2,1)} %collective-permute-done.1.refs_1_, bf16[2048,128]{1,0:T(8,128)(2,1)} %collective-permute-done.2.refs_2_, ...), custom_call_target="tpu_custom_call" | custom-call | flops 1073741824 | bytes 8388608 | tf_op jit(solution)/shard_map/project/pallas_call | solution.py:139
  (34 shorter events, 1.8 us)
Async XLA Ops:
  0.0 2.3 %copy-start = (bf16[128,2048]{1,0:T(8,128)(2,1)S(1)}, bf16[128,2048]{1,0:T(8,128)(2,1)}, u32[]{:S(2)}) copy-start(bf16[128,2048]{1,0:T(8,128)(2,1)} %param.8) | copy-start | bytes 1572868
  0.0 1.7 %copy-start.5 = (bf16[128,2048]{1,0:T(8,128)(2,1)S(1)}, bf16[128,2048]{1,0:T(8,128)(2,1)}, u32[]{:S(2)}) copy-start(bf16[128,2048]{1,0:T(8,128)(2,1)} %param.7) | copy-start | bytes 1572868
  51.7 20.5 %collective-permute-start.4 = (bf16[2048,128]{1,0:T(8,128)(2,1)S(1)}, bf16[2048,128]{1,0:T(8,128)(2,1)S(1)}, u32[]{:S(2)}, u32[]{:S(2)}) collective-permute-start(bf16[2048,128]{1,0:T(8,128)(2,1)S(1)} %bitcast.11), channel_id=1, source_target_pairs={{0,32},{16,48},{32,64},{48,80},{64,96},{80,112},{96,0},{112,16},{1... | collective-permute-start | bytes 1572872 | tf_op jit(solution)/shard_map/ppermute | solution.py:189
  54.2 20.5 %copy-start.6 = (s32[2048]{0:T(1024)S(1)}, s32[2048]{0:T(1024)}, u32[]{:S(2)}) copy-start(s32[2048]{0:T(1024)} %param.9) | copy-start | bytes 24580
  54.2 58.3 %collective-permute-start = (bf16[16,2,128,128]{3,2,1,0:T(8,128)(2,1)}, bf16[16,2,128,128]{3,2,1,0:T(8,128)(2,1)}, u32[]{:S(2)}, u32[]{:S(2)}) collective-permute-start(bf16[16,2,128,128]{3,2,1,0:T(8,128)(2,1)} %slice.8), channel_id=1, source_target_pairs={{0,16},{16,32},{32,48},{48,64},{64,80},{80,96},{96,112},{112,128},... | collective-permute-start | bytes 3145736 | tf_op jit(solution)/shard_map/ppermute | solution.py:180
  64.6 48.2 %all-to-all-start = ((bf16[16,128,128]{2,1,0:T(8,128)(2,1)}), bf16[16,128,128]{2,1,0:T(8,128)(2,1)}, u32[]{:S(2)}, u32[]{:S(2)}) async-start(bf16[16,128,128]{2,1,0:T(8,128)(2,1)} %bitcast.18), calls=%async_computation | async-start | bytes 1048576 | tf_op jit(solution)/shard_map/all_to_all | solution.py:182
  68.9 19.9 %collective-permute-start.10 = (bf16[2048,128]{1,0:T(8,128)(2,1)S(1)}, bf16[2048,128]{1,0:T(8,128)(2,1)}, u32[]{:S(2)}, u32[]{:S(2)}) collective-permute-start(bf16[2048,128]{1,0:T(8,128)(2,1)S(1)} %bitcast.12), channel_id=1, source_target_pairs={{0,224},{16,240},{32,128},{48,144},{64,160},{80,176},{96,192},{112... | collective-permute-start | bytes 1572872 | tf_op jit(solution)/shard_map/ppermute | solution.py:189
  69.0 30.7 %collective-permute-start.2 = (bf16[2048,128]{1,0:T(8,128)(2,1)S(1)}, bf16[2048,128]{1,0:T(8,128)(2,1)}, u32[]{:S(2)}, u32[]{:S(2)}) collective-permute-start(bf16[2048,128]{1,0:T(8,128)(2,1)S(1)} %bitcast.13), channel_id=1, source_target_pairs={{0,128},{16,144},{32,160},{48,176},{64,192},{80,208},{96,224},{112... | collective-permute-start | bytes 1572872 | tf_op jit(solution)/shard_map/ppermute | solution.py:189
  72.2 38.0 %collective-permute-start.6 = (bf16[2048,128]{1,0:T(8,128)(2,1)S(1)}, bf16[2048,128]{1,0:T(8,128)(2,1)}, u32[]{:S(2)}, u32[]{:S(2)}) collective-permute-start(bf16[2048,128]{1,0:T(8,128)(2,1)S(1)} %bitcast.14), channel_id=1, source_target_pairs={{0,160},{16,176},{32,192},{48,208},{64,224},{80,240},{96,128},{112... | collective-permute-start | bytes 1572872 | tf_op jit(solution)/shard_map/ppermute | solution.py:189
  72.2 38.9 %collective-permute-start.8 = (bf16[2048,128]{1,0:T(8,128)(2,1)S(1)}, bf16[2048,128]{1,0:T(8,128)(2,1)}, u32[]{:S(2)}, u32[]{:S(2)}) collective-permute-start(bf16[2048,128]{1,0:T(8,128)(2,1)S(1)} %bitcast.15), channel_id=1, source_target_pairs={{0,96},{16,112},{32,0},{48,16},{64,32},{80,48},{96,64},{112,80},{1... | collective-permute-start | bytes 1572872 | tf_op jit(solution)/shard_map/ppermute | solution.py:189
  88.8 53.4 %collective-permute-start.1 = (bf16[2048,128]{1,0:T(8,128)(2,1)S(1)}, bf16[2048,128]{1,0:T(8,128)(2,1)}, u32[]{:S(2)}, u32[]{:S(2)}) collective-permute-start(bf16[2048,128]{1,0:T(8,128)(2,1)S(1)} %bitcast.16), channel_id=1, source_target_pairs={{0,16},{16,0},{32,48},{48,32},{64,80},{80,64},{96,112},{112,96},{1... | collective-permute-start | bytes 1572872 | tf_op jit(solution)/shard_map/ppermute | solution.py:199
  99.7 43.4 %collective-permute-start.14 = (bf16[2048,128]{1,0:T(8,128)(2,1)}, bf16[2048,128]{1,0:T(8,128)(2,1)}, u32[]{:S(2)}, u32[]{:S(2)}) collective-permute-start(bf16[2048,128]{1,0:T(8,128)(2,1)} %collective-permute-done.10.refs_10_), channel_id=1, source_target_pairs={{0,96},{16,112},{32,0},{48,16},{64,32},{80,48},{96,64},{112,80},{1... | collective-permute-start | bytes 1572872 | tf_op jit(solution)/shard_map/ppermute | solution.py:189
  110.2 33.1 %collective-permute-start.11 = (bf16[2048,128]{1,0:T(8,128)(2,1)}, bf16[2048,128]{1,0:T(8,128)(2,1)}, u32[]{:S(2)}, u32[]{:S(2)}) collective-permute-start(bf16[2048,128]{1,0:T(8,128)(2,1)} %collective-permute-done.10.refs_10_), channel_id=1, source_target_pairs={{0,16},{16,0},{32,48},{48,32},{64,80},{80,64},{96,112},{112,96},{1... | collective-permute-start | bytes 1572872 | tf_op jit(solution)/shard_map/ppermute | solution.py:199
  111.1 31.7 %collective-permute-start.12 = (bf16[2048,128]{1,0:T(8,128)(2,1)S(1)}, bf16[2048,128]{1,0:T(8,128)(2,1)}, u32[]{:S(2)}, u32[]{:S(2)}) collective-permute-start(bf16[2048,128]{1,0:T(8,128)(2,1)S(1)} %collective-permute-done.4.refs_4_), channel_id=1, source_target_pairs={{0,32},{16,48},{32,64},{48,80},{64,96},{80,112},{96,0},{112,16},{1... | collective-permute-start | bytes 1572872 | tf_op jit(solution)/shard_map/ppermute | solution.py:189
  112.4 31.1 %collective-permute-start.5 = (bf16[2048,128]{1,0:T(8,128)(2,1)S(1)}, bf16[2048,128]{1,0:T(8,128)(2,1)}, u32[]{:S(2)}, u32[]{:S(2)}) collective-permute-start(bf16[2048,128]{1,0:T(8,128)(2,1)S(1)} %collective-permute-done.4.refs_4_), channel_id=1, source_target_pairs={{0,16},{16,0},{32,48},{48,32},{64,80},{80,64},{96,112},{112,96},{1... | collective-permute-start | bytes 1572872 | tf_op jit(solution)/shard_map/ppermute | solution.py:199
  133.2 0.8 copy-start.1
  134.0 24.2 %all-to-all-start.2 = ((bf16[16,128,128]{2,1,0:T(8,128)(2,1)}), bf16[16,128,128]{2,1,0:T(8,128)(2,1)S(1)}, u32[]{:S(2)}, u32[]{:S(2)}) async-start(bf16[16,128,128]{2,1,0:T(8,128)(2,1)} %copy-done.1), calls=%async_computation.2 | async-start | bytes 1048576 | tf_op jit(solution)/shard_map/all_to_all | solution.py:206
  142.3 2.4 %collective-permute-start.3 = (bf16[2048,128]{1,0:T(8,128)(2,1)}, bf16[2048,128]{1,0:T(8,128)(2,1)S(1)}, u32[]{:S(2)}, u32[]{:S(2)}) collective-permute-start(bf16[2048,128]{1,0:T(8,128)(2,1)} %collective-permute-done.2.refs_2_), channel_id=1, source_target_pairs={{0,16},{16,0},{32,48},{48,32},{64,80},{80,64},{96,112},{112,96},{1... | collective-permute-start | bytes 1572872 | tf_op jit(solution)/shard_map/ppermute | solution.py:199
  142.8 2.6 %collective-permute-start.7 = (bf16[2048,128]{1,0:T(8,128)(2,1)}, bf16[2048,128]{1,0:T(8,128)(2,1)S(1)}, u32[]{:S(2)}, u32[]{:S(2)}) collective-permute-start(bf16[2048,128]{1,0:T(8,128)(2,1)} %collective-permute-done.6.refs_6_), channel_id=1, source_target_pairs={{0,16},{16,0},{32,48},{48,32},{64,80},{80,64},{96,112},{112,96},{1... | collective-permute-start | bytes 1572872 | tf_op jit(solution)/shard_map/ppermute | solution.py:199
  143.0 3.1 %collective-permute-start.9 = (bf16[2048,128]{1,0:T(8,128)(2,1)}, bf16[2048,128]{1,0:T(8,128)(2,1)S(1)}, u32[]{:S(2)}, u32[]{:S(2)}) collective-permute-start(bf16[2048,128]{1,0:T(8,128)(2,1)} %collective-permute-done.8.refs_8_), channel_id=1, source_target_pairs={{0,16},{16,0},{32,48},{48,32},{64,80},{80,64},{96,112},{112,96},{1... | collective-permute-start | bytes 1572872 | tf_op jit(solution)/shard_map/ppermute | solution.py:199
  143.3 3.6 %collective-permute-start.13 = (bf16[2048,128]{1,0:T(8,128)(2,1)}, bf16[2048,128]{1,0:T(8,128)(2,1)S(1)}, u32[]{:S(2)}, u32[]{:S(2)}) collective-permute-start(bf16[2048,128]{1,0:T(8,128)(2,1)} %collective-permute-done.12.refs_12_), channel_id=1, source_target_pairs={{0,16},{16,0},{32,48},{48,32},{64,80},{80,64},{96,112},{112,96},{1... | collective-permute-start | bytes 1572872 | tf_op jit(solution)/shard_map/ppermute | solution.py:199
  143.6 4.2 %collective-permute-start.15 = (bf16[2048,128]{1,0:T(8,128)(2,1)}, bf16[2048,128]{1,0:T(8,128)(2,1)}, u32[]{:S(2)}, u32[]{:S(2)}) collective-permute-start(bf16[2048,128]{1,0:T(8,128)(2,1)} %collective-permute-done.14.refs_14_), channel_id=1, source_target_pairs={{0,16},{16,0},{32,48},{48,32},{64,80},{80,64},{96,112},{112,96},{1... | collective-permute-start | bytes 1572872 | tf_op jit(solution)/shard_map/ppermute | solution.py:199
  145.4 12.8 %copy-start.2 = (bf16[2048,128]{1,0:T(8,128)(2,1)}, bf16[2048,128]{1,0:T(8,128)(2,1)S(1)}, u32[]{:S(2)}) copy-start(bf16[2048,128]{1,0:T(8,128)(2,1)S(1)} %collective-permute-done.7.refs_7_) | copy-start | bytes 1572868
  146.1 0.8 copy-start.3
  146.9 0.8 copy-start.4

commit v4 on v3

--- a/solution.py
+++ b/solution.py
@@ -63,17 +63,16 @@
             top = jnp.maximum(s[:, :LANES], s[:, LANES:])
             largest = top if largest is None else jnp.maximum(largest, top)
         shift = jnp.max(largest, axis=1, keepdims=True) * factor
-        total = None
         acc = None
         for kb in range(blocks):
             values = vbuf[pl.ds(per_tile * (t + kb), per_tile)].reshape(TILE, LANES)
             p = jnp.exp2(s_ref[head, kb] * factor - shift)
-            part = p[:, :LANES] + p[:, LANES:]
-            total = part if total is None else total + part
+            values = jnp.where(mine, values, jnp.ones_like(values))
             term = jnp.dot(p.astype(jnp.bfloat16), values, preferred_element_type=jnp.float32)
             acc = term if acc is None else acc + term
-        outs.append(acc / jnp.sum(total, axis=1, keepdims=True))
-    out = jnp.where(lane < HEAD_DIM, outs[0], outs[1])
+        outs.append(acc)
+    total = pltpu.roll(jnp.where(lane < HEAD_DIM, outs[1], outs[0]), HEAD_DIM, 1)
+    out = jnp.where(lane < HEAD_DIM, outs[0], outs[1]) / total
     o_ref[...] = out.astype(jnp.bfloat16).reshape(o_ref.shape)
 
 

time: 165 us -> 164 us (level)
  no operation moved by 1% of the time
where the time goes in v4:
time: 164 us; the launch traced here: 163 us
  blocking collectives  49.1 us (30%)
  waiting for transfers between devices  43.8 us (27%)
  starting transfers between devices  35.4 us (22%)
  Pallas kernels  24.6 us (15%)
  local copies, waits for them, and re-layouts  9.49 us (6%)
    all_to_all x1, blocking collectives, layer(): lax.all_to_all(jnp.stack([split(key_rows), split(value_rows), jnp.broadca...  49.1 us
    ppermute x7, waiting for transfers between devices, shift(): return lax.ppermute(x, 'blk', pairs)  30.3 us
    pallas_call x1, Pallas kernels, attention(): pl.pallas_call(attend_kernel, grid=(tiles,), out_shape=jax.ShapeDtypeStru...  19.2 us
    ppermute x7, starting transfers between devices, shift(): return lax.ppermute(x, 'blk', pairs)  13.2 us
    all_to_all x1, waiting for transfers between devices, layer(): ctx = lax.all_to_all(ctx, 'head', 0, 0, tiled=True)  10.4 us
    all_to_all x1, starting transfers between devices, layer(): ctx = lax.all_to_all(ctx, 'head', 0, 0, tiled=True)  8.26 us
    ppermute x1, starting transfers between devices, layer(): lax.ppermute(kvw[:, :2], 'blk', [(i, i + 1) for i in range(blks - 1)])  6.33 us
    pallas_call x1, Pallas kernels, project(): pl.pallas_call(functools.partial(project_kernel, shifts=shifts), out_shap...  5.43 us
  transfers between devices with their start and end apart: 18, of which 8 were waited for; matrix products, arithmetic and copies ran while one was open for 3% of the time, Pallas kernels for 12%

profile of v4, /device:TPU:1, one launch (start us, length us, event | category | flops | bytes accessed | tf_op | source)
XLA Modules:
  0.0 162.9 jit_solution(13825157422660167853)
XLA Ops:
  0.0 1.4 copy.8
  1.4 0.3 copy.9
  2.0 0.3 copy.11
  2.6 49.1 %all_to_all.15.own_ref = bf16[16,3,128,128]{3,2,1,0:T(8,128)(2,1)S(1)} all-to-all(bf16[16,3,128,128]{3,2,1,0:T(8,128)(2,1)S(1)} %pad_maximum_fusion), channel_id=1, replica_groups=mesh['blk'=16,'head'=16] {'head'}, dimensions={0} | all-to-all | bytes 3145728 | tf_op jit(solution)/shard_map/all_to_all | solution.py:165
  51.7 1.4 collective-permute-start.4
  53.1 1.0 slice.8
  54.2 6.3 %collective-permute-start = (bf16[16,2,128,128]{3,2,1,0:T(8,128)(2,1)}, bf16[16,2,128,128]{3,2,1,0:T(8,128)(2,1)}, u32[]{:S(2)}, u32[]{:S(2)}) collective-permute-start(bf16[16,2,128,128]{3,2,1,0:T(8,128)(2,1)} %slice.8), channel_id=1, source_target_pairs={{0,16},{16,32},{32,48},{48,64},{64,80},{80,96},{96,112},{112,128},... | collective-permute-start | bytes 3145736 | tf_op jit(solution)/shard_map/ppermute | solution.py:179
  60.5 2.0 %copy.6 = bf16[128,2048]{0,1:T(8,128)(2,1)} copy(bf16[128,2048]{1,0:T(8,128)(2,1)} %param.5) | data formatting | bytes 1048576 | tf_op args[0]
  62.5 2.0 %copy.7 = bf16[128,16,128]{2,0,1:T(8,128)(2,1)} copy(bf16[128,16,128]{0,2,1:T(8,128)(2,1)} %bitcast.21) | data formatting | bytes 1048576 | tf_op jit(solution)/shard_map/reshape | solution.py:162
  64.6 4.4 %all-to-all-start = ((bf16[16,128,128]{2,1,0:T(8,128)(2,1)}), bf16[16,128,128]{2,1,0:T(8,128)(2,1)}, u32[]{:S(2)}, u32[]{:S(2)}) async-start(bf16[16,128,128]{2,1,0:T(8,128)(2,1)} %bitcast.18), calls=%async_computation | async-start | bytes 1048576 | tf_op jit(solution)/shard_map/all_to_all | solution.py:181
  69.0 3.2 %collective-permute-start.2 = (bf16[2048,128]{1,0:T(8,128)(2,1)S(1)}, bf16[2048,128]{1,0:T(8,128)(2,1)}, u32[]{:S(2)}, u32[]{:S(2)}) collective-permute-start(bf16[2048,128]{1,0:T(8,128)(2,1)S(1)} %bitcast.13), channel_id=1, source_target_pairs={{0,128},{16,144},{32,160},{48,176},{64,192},{80,208},{96,224},{112... | collective-permute-start | bytes 1572872 | tf_op jit(solution)/shard_map/ppermute | solution.py:188
  72.2 2.4 %collective-permute-start.8 = (bf16[2048,128]{1,0:T(8,128)(2,1)S(1)}, bf16[2048,128]{1,0:T(8,128)(2,1)}, u32[]{:S(2)}, u32[]{:S(2)}) collective-permute-start(bf16[2048,128]{1,0:T(8,128)(2,1)S(1)} %bitcast.15), channel_id=1, source_target_pairs={{0,96},{16,112},{32,0},{48,16},{64,32},{80,48},{96,64},{112,80},{1... | collective-permute-start | bytes 1572872 | tf_op jit(solution)/shard_map/ppermute | solution.py:188
  74.6 14.2 %collective-permute-done.10.refs_10_ = bf16[2048,128]{1,0:T(8,128)(2,1)} collective-permute-done((bf16[2048,128]{1,0:T(8,128)(2,1)S(1)}, bf16[2048,128]{1,0:T(8,128)(2,1)}, u32[]{:S(2)}, u32[]{:S(2)}) %collective-permute-start.10) | collective-permute-done | bytes 524320 | tf_op jit(solution)/shard_map/ppermute | solution.py:188
  88.8 0.5 collective-permute-start.1
  89.3 10.4 %collective-permute-done.2.refs_2_ = bf16[2048,128]{1,0:T(8,128)(2,1)} collective-permute-done((bf16[2048,128]{1,0:T(8,128)(2,1)S(1)}, bf16[2048,128]{1,0:T(8,128)(2,1)}, u32[]{:S(2)}, u32[]{:S(2)}) %collective-permute-start.2) | collective-permute-done | bytes 524320 | tf_op jit(solution)/shard_map/ppermute | solution.py:188
  99.7 4.8 %collective-permute-start.14 = (bf16[2048,128]{1,0:T(8,128)(2,1)}, bf16[2048,128]{1,0:T(8,128)(2,1)}, u32[]{:S(2)}, u32[]{:S(2)}) collective-permute-start(bf16[2048,128]{1,0:T(8,128)(2,1)} %collective-permute-done.10.refs_10_), channel_id=1, source_target_pairs={{0,96},{16,112},{32,0},{48,16},{64,32},{80,48},{96,64},{112,80},{1... | collective-permute-start | bytes 1572872 | tf_op jit(solution)/shard_map/ppermute | solution.py:188
  104.5 5.7 %collective-permute-done.6.refs_6_ = bf16[2048,128]{1,0:T(8,128)(2,1)} collective-permute-done((bf16[2048,128]{1,0:T(8,128)(2,1)S(1)}, bf16[2048,128]{1,0:T(8,128)(2,1)}, u32[]{:S(2)}, u32[]{:S(2)}) %collective-permute-start.6) | collective-permute-done | bytes 524320 | tf_op jit(solution)/shard_map/ppermute | solution.py:188
  110.2 0.9 collective-permute-start.11
  111.1 1.3 collective-permute-start.12
  112.4 0.4 collective-permute-start.5
  112.8 0.3 broadcast_in_dim.2.low_ref
  113.2 19.2 %attend.1 = bf16[16,128,128]{2,1,0:T(8,128)(2,1)S(1)} custom-call(s32[2048,128]{1,0:T(8,128)S(1)} %broadcast_in_dim.2.low_ref, bf16[16,128,128]{2,1,0:T(8,128)(2,1)} %all-to-all-done.q_ref, bf16[16,3,128,128]{3,2,1,0:T(8,128)(2,1)S(1)} %all_to_all.15.own_ref, bf16[16,2,128,128]{3,2,1,0:T(8,128)(2,1)} %collective-permute-done.prev_ref), custom_call_target="tpu_custom_call" | custom-call | flops 4831838208 | bytes 3145728 | tf_op jit(solution)/shard_map/attend/pallas_call | solution.py:84
  132.4 0.8 copy-done.1
  133.2 8.3 %all-to-all-start.2 = ((bf16[16,128,128]{2,1,0:T(8,128)(2,1)}), bf16[16,128,128]{2,1,0:T(8,128)(2,1)S(1)}, u32[]{:S(2)}, u32[]{:S(2)}) async-start(bf16[16,128,128]{2,1,0:T(8,128)(2,1)} %copy-done.1), calls=%async_computation.2 | async-start | bytes 1048576 | tf_op jit(solution)/shard_map/all_to_all | solution.py:205
  141.4 0.5 collective-permute-start.3
  143.0 0.8 collective-permute-done.3.refs_3_
  143.8 0.7 collective-permute-done.7.refs_7_
  144.6 0.7 collective-permute-done.9.refs_9_
  145.3 0.7 collective-permute-done.13.refs_13_
  146.1 0.8 copy-done.4
  147.0 10.4 %all-to-all-done.2.ctx_ref = bf16[16,128,128]{2,1,0:T(8,128)(2,1)S(1)} async-done(((bf16[16,128,128]{2,1,0:T(8,128)(2,1)}), bf16[16,128,128]{2,1,0:T(8,128)(2,1)S(1)}, u32[]{:S(2)}, u32[]{:S(2)}) %all-to-all-start.2) | async-done | bytes 524320 | tf_op jit(solution)/shard_map/all_to_all | solution.py:205
  157.4 5.4 %project.1 = bf16[128,2048]{1,0:T(8,128)(2,1)} custom-call(bf16[16,128,128]{2,1,0:T(8,128)(2,1)S(1)} %all-to-all-done.2.ctx_ref, bf16[2048,128]{1,0:T(8,128)(2,1)S(1)} %bitcast.17, bf16[2048,128]{1,0:T(8,128)(2,1)} %collective-permute-done.1.refs_1_, bf16[2048,128]{1,0:T(8,128)(2,1)} %collective-permute-done.2.refs_2_, ...), custom_call_target="tpu_custom_call" | custom-call | flops 1073741824 | bytes 8388608 | tf_op jit(solution)/shard_map/project/pallas_call | solution.py:138
  (34 shorter events, 1.8 us)
Async XLA Ops:
  0.0 2.3 %copy-start = (bf16[128,2048]{1,0:T(8,128)(2,1)S(1)}, bf16[128,2048]{1,0:T(8,128)(2,1)}, u32[]{:S(2)}) copy-start(bf16[128,2048]{1,0:T(8,128)(2,1)} %param.8) | copy-start | bytes 1572868
  0.0 1.7 %copy-start.5 = (bf16[128,2048]{1,0:T(8,128)(2,1)S(1)}, bf16[128,2048]{1,0:T(8,128)(2,1)}, u32[]{:S(2)}) copy-start(bf16[128,2048]{1,0:T(8,128)(2,1)} %param.7) | copy-start | bytes 1572868
  51.7 20.5 %collective-permute-start.4 = (bf16[2048,128]{1,0:T(8,128)(2,1)S(1)}, bf16[2048,128]{1,0:T(8,128)(2,1)S(1)}, u32[]{:S(2)}, u32[]{:S(2)}) collective-permute-start(bf16[2048,128]{1,0:T(8,128)(2,1)S(1)} %bitcast.11), channel_id=1, source_target_pairs={{0,32},{16,48},{32,64},{48,80},{64,96},{80,112},{96,0},{112,16},{1... | collective-permute-start | bytes 1572872 | tf_op jit(solution)/shard_map/ppermute | solution.py:188
  54.2 20.5 %copy-start.6 = (s32[2048]{0:T(1024)S(1)}, s32[2048]{0:T(1024)}, u32[]{:S(2)}) copy-start(s32[2048]{0:T(1024)} %param.9) | copy-start | bytes 24580
  54.2 58.3 %collective-permute-start = (bf16[16,2,128,128]{3,2,1,0:T(8,128)(2,1)}, bf16[16,2,128,128]{3,2,1,0:T(8,128)(2,1)}, u32[]{:S(2)}, u32[]{:S(2)}) collective-permute-start(bf16[16,2,128,128]{3,2,1,0:T(8,128)(2,1)} %slice.8), channel_id=1, source_target_pairs={{0,16},{16,32},{32,48},{48,64},{64,80},{80,96},{96,112},{112,128},... | collective-permute-start | bytes 3145736 | tf_op jit(solution)/shard_map/ppermute | solution.py:179
  64.6 48.2 %all-to-all-start = ((bf16[16,128,128]{2,1,0:T(8,128)(2,1)}), bf16[16,128,128]{2,1,0:T(8,128)(2,1)}, u32[]{:S(2)}, u32[]{:S(2)}) async-start(bf16[16,128,128]{2,1,0:T(8,128)(2,1)} %bitcast.18), calls=%async_computation | async-start | bytes 1048576 | tf_op jit(solution)/shard_map/all_to_all | solution.py:181
  68.9 19.9 %collective-permute-start.10 = (bf16[2048,128]{1,0:T(8,128)(2,1)S(1)}, bf16[2048,128]{1,0:T(8,128)(2,1)}, u32[]{:S(2)}, u32[]{:S(2)}) collective-permute-start(bf16[2048,128]{1,0:T(8,128)(2,1)S(1)} %bitcast.12), channel_id=1, source_target_pairs={{0,224},{16,240},{32,128},{48,144},{64,160},{80,176},{96,192},{112... | collective-permute-start | bytes 1572872 | tf_op jit(solution)/shard_map/ppermute | solution.py:188
  69.0 30.7 %collective-permute-start.2 = (bf16[2048,128]{1,0:T(8,128)(2,1)S(1)}, bf16[2048,128]{1,0:T(8,128)(2,1)}, u32[]{:S(2)}, u32[]{:S(2)}) collective-permute-start(bf16[2048,128]{1,0:T(8,128)(2,1)S(1)} %bitcast.13), channel_id=1, source_target_pairs={{0,128},{16,144},{32,160},{48,176},{64,192},{80,208},{96,224},{112... | collective-permute-start | bytes 1572872 | tf_op jit(solution)/shard_map/ppermute | solution.py:188
  72.2 38.0 %collective-permute-start.6 = (bf16[2048,128]{1,0:T(8,128)(2,1)S(1)}, bf16[2048,128]{1,0:T(8,128)(2,1)}, u32[]{:S(2)}, u32[]{:S(2)}) collective-permute-start(bf16[2048,128]{1,0:T(8,128)(2,1)S(1)} %bitcast.14), channel_id=1, source_target_pairs={{0,160},{16,176},{32,192},{48,208},{64,224},{80,240},{96,128},{112... | collective-permute-start | bytes 1572872 | tf_op jit(solution)/shard_map/ppermute | solution.py:188
  72.2 38.9 %collective-permute-start.8 = (bf16[2048,128]{1,0:T(8,128)(2,1)S(1)}, bf16[2048,128]{1,0:T(8,128)(2,1)}, u32[]{:S(2)}, u32[]{:S(2)}) collective-permute-start(bf16[2048,128]{1,0:T(8,128)(2,1)S(1)} %bitcast.15), channel_id=1, source_target_pairs={{0,96},{16,112},{32,0},{48,16},{64,32},{80,48},{96,64},{112,80},{1... | collective-permute-start | bytes 1572872 | tf_op jit(solution)/shard_map/ppermute | solution.py:188
  88.8 52.6 %collective-permute-start.1 = (bf16[2048,128]{1,0:T(8,128)(2,1)S(1)}, bf16[2048,128]{1,0:T(8,128)(2,1)}, u32[]{:S(2)}, u32[]{:S(2)}) collective-permute-start(bf16[2048,128]{1,0:T(8,128)(2,1)S(1)} %bitcast.16), channel_id=1, source_target_pairs={{0,16},{16,0},{32,48},{48,32},{64,80},{80,64},{96,112},{112,96},{1... | collective-permute-start | bytes 1572872 | tf_op jit(solution)/shard_map/ppermute | solution.py:198
  99.7 42.5 %collective-permute-start.14 = (bf16[2048,128]{1,0:T(8,128)(2,1)}, bf16[2048,128]{1,0:T(8,128)(2,1)}, u32[]{:S(2)}, u32[]{:S(2)}) collective-permute-start(bf16[2048,128]{1,0:T(8,128)(2,1)} %collective-permute-done.10.refs_10_), channel_id=1, source_target_pairs={{0,96},{16,112},{32,0},{48,16},{64,32},{80,48},{96,64},{112,80},{1... | collective-permute-start | bytes 1572872 | tf_op jit(solution)/shard_map/ppermute | solution.py:188
  110.2 32.3 %collective-permute-start.11 = (bf16[2048,128]{1,0:T(8,128)(2,1)}, bf16[2048,128]{1,0:T(8,128)(2,1)}, u32[]{:S(2)}, u32[]{:S(2)}) collective-permute-start(bf16[2048,128]{1,0:T(8,128)(2,1)} %collective-permute-done.10.refs_10_), channel_id=1, source_target_pairs={{0,16},{16,0},{32,48},{48,32},{64,80},{80,64},{96,112},{112,96},{1... | collective-permute-start | bytes 1572872 | tf_op jit(solution)/shard_map/ppermute | solution.py:198
  111.1 30.8 %collective-permute-start.12 = (bf16[2048,128]{1,0:T(8,128)(2,1)S(1)}, bf16[2048,128]{1,0:T(8,128)(2,1)}, u32[]{:S(2)}, u32[]{:S(2)}) collective-permute-start(bf16[2048,128]{1,0:T(8,128)(2,1)S(1)} %collective-permute-done.4.refs_4_), channel_id=1, source_target_pairs={{0,32},{16,48},{32,64},{48,80},{64,96},{80,112},{96,0},{112,16},{1... | collective-permute-start | bytes 1572872 | tf_op jit(solution)/shard_map/ppermute | solution.py:188
  112.4 30.3 %collective-permute-start.5 = (bf16[2048,128]{1,0:T(8,128)(2,1)S(1)}, bf16[2048,128]{1,0:T(8,128)(2,1)}, u32[]{:S(2)}, u32[]{:S(2)}) collective-permute-start(bf16[2048,128]{1,0:T(8,128)(2,1)S(1)} %collective-permute-done.4.refs_4_), channel_id=1, source_target_pairs={{0,16},{16,0},{32,48},{48,32},{64,80},{80,64},{96,112},{112,96},{1... | collective-permute-start | bytes 1572872 | tf_op jit(solution)/shard_map/ppermute | solution.py:198
  132.4 0.8 copy-start.1
  133.2 24.2 %all-to-all-start.2 = ((bf16[16,128,128]{2,1,0:T(8,128)(2,1)}), bf16[16,128,128]{2,1,0:T(8,128)(2,1)S(1)}, u32[]{:S(2)}, u32[]{:S(2)}) async-start(bf16[16,128,128]{2,1,0:T(8,128)(2,1)} %copy-done.1), calls=%async_computation.2 | async-start | bytes 1048576 | tf_op jit(solution)/shard_map/all_to_all | solution.py:205
  141.4 2.4 %collective-permute-start.3 = (bf16[2048,128]{1,0:T(8,128)(2,1)}, bf16[2048,128]{1,0:T(8,128)(2,1)S(1)}, u32[]{:S(2)}, u32[]{:S(2)}) collective-permute-start(bf16[2048,128]{1,0:T(8,128)(2,1)} %collective-permute-done.2.refs_2_), channel_id=1, source_target_pairs={{0,16},{16,0},{32,48},{48,32},{64,80},{80,64},{96,112},{112,96},{1... | collective-permute-start | bytes 1572872 | tf_op jit(solution)/shard_map/ppermute | solution.py:198
  142.0 2.6 %collective-permute-start.7 = (bf16[2048,128]{1,0:T(8,128)(2,1)}, bf16[2048,128]{1,0:T(8,128)(2,1)S(1)}, u32[]{:S(2)}, u32[]{:S(2)}) collective-permute-start(bf16[2048,128]{1,0:T(8,128)(2,1)} %collective-permute-done.6.refs_6_), channel_id=1, source_target_pairs={{0,16},{16,0},{32,48},{48,32},{64,80},{80,64},{96,112},{112,96},{1... | collective-permute-start | bytes 1572872 | tf_op jit(solution)/shard_map/ppermute | solution.py:198
  142.2 3.1 %collective-permute-start.9 = (bf16[2048,128]{1,0:T(8,128)(2,1)}, bf16[2048,128]{1,0:T(8,128)(2,1)S(1)}, u32[]{:S(2)}, u32[]{:S(2)}) collective-permute-start(bf16[2048,128]{1,0:T(8,128)(2,1)} %collective-permute-done.8.refs_8_), channel_id=1, source_target_pairs={{0,16},{16,0},{32,48},{48,32},{64,80},{80,64},{96,112},{112,96},{1... | collective-permute-start | bytes 1572872 | tf_op jit(solution)/shard_map/ppermute | solution.py:198
  142.5 3.6 %collective-permute-start.13 = (bf16[2048,128]{1,0:T(8,128)(2,1)}, bf16[2048,128]{1,0:T(8,128)(2,1)S(1)}, u32[]{:S(2)}, u32[]{:S(2)}) collective-permute-start(bf16[2048,128]{1,0:T(8,128)(2,1)} %collective-permute-done.12.refs_12_), channel_id=1, source_target_pairs={{0,16},{16,0},{32,48},{48,32},{64,80},{80,64},{96,112},{112,96},{1... | collective-permute-start | bytes 1572872 | tf_op jit(solution)/shard_map/ppermute | solution.py:198
  142.7 4.2 %collective-permute-start.15 = (bf16[2048,128]{1,0:T(8,128)(2,1)}, bf16[2048,128]{1,0:T(8,128)(2,1)}, u32[]{:S(2)}, u32[]{:S(2)}) collective-permute-start(bf16[2048,128]{1,0:T(8,128)(2,1)} %collective-permute-done.14.refs_14_), channel_id=1, source_target_pairs={{0,16},{16,0},{32,48},{48,32},{64,80},{80,64},{96,112},{112,96},{1... | collective-permute-start | bytes 1572872 | tf_op jit(solution)/shard_map/ppermute | solution.py:198
  144.6 12.8 %copy-start.2 = (bf16[2048,128]{1,0:T(8,128)(2,1)}, bf16[2048,128]{1,0:T(8,128)(2,1)S(1)}, u32[]{:S(2)}) copy-start(bf16[2048,128]{1,0:T(8,128)(2,1)S(1)} %collective-permute-done.7.refs_7_) | copy-start | bytes 1572868
  145.3 0.8 copy-start.3
  146.1 0.8 copy-start.4
